TPU v7x, 32 devices: a whole 2x2x4 slice. The times are simulated.
32 devices in a mesh: groups: 2 (over y), roll: 4 (over z), tp: 2 (over x), seq: 2 (over core).
Axes of the slice: x: 2, y: 2, z: 4, core: 2. Of those that a mesh axis runs over, the one named last changes fastest.
Arguments:
- hidden: bfloat16 [128, 8192], P('groups', ('roll', 'seq')), parts along dimension 0, may hold values from -6 to 6
- w_query: bfloat16 [8192, 8192], P(('roll', 'seq'), 'tp'), may hold values from -0.0625 to 0.0625
- w_key: bfloat16 [8192, 1024], P(('roll', 'seq'), 'tp'), may hold values from -0.0625 to 0.0625
- w_value: bfloat16 [8192, 1024], P(('roll', 'seq'), 'tp'), may hold values from -0.0625 to 0.0625
- b_query: bfloat16 [8192], P('tp'), may hold values from -12 to 12
- b_key: bfloat16 [1024], P('tp'), may hold values from -12 to 12
- b_value: bfloat16 [1024], P('tp'), may hold values from -6 to 6
- w_out: bfloat16 [8192, 8192], P('tp', ('roll', 'seq')), may hold values from -0.0625 to 0.0625
- prefix_keys: bfloat16 [4, 4096, 1024], P('groups', ('roll', 'seq'), 'tp'), parts along dimension 0, may hold values from -256 to 256
- prefix_values: bfloat16 [4, 4096, 1024], P('groups', ('roll', 'seq'), 'tp'), parts along dimension 0, may hold values from -6 to 6
- suffix_keys: bfloat16 [16, 2048, 1024], P(('groups', 'roll'), 'seq', 'tp'), parts along dimension 0, may hold values from -6 to 6
- suffix_values: bfloat16 [16, 2048, 1024], P(('groups', 'roll'), 'seq', 'tp'), parts along dimension 0, may hold values from -6 to 6
- suffix_lengths: int32 [16], P('groups'), parts along dimension 0, may hold values from 1 to 2048, 8192 in all
- prompt_of: int32 [16], P('groups'), parts along dimension 0, may hold values from 0 to 1, as said below
Outputs:
- attended: bfloat16 [128, 8192], P(('groups', 'tp'), ('roll', 'seq')), parts along dimension 0
There are 2 independent parts, one for each index of `groups`. A program takes and returns all parts, laid end to end along the dimension named above; an argument that names none is the same for every part. Nothing has to cross between parts.
Inputs may be any that keep to these rules, and one draw needn't show every extreme that they name: Only the first suffix_lengths[r] rows of a rollout's suffix cache are live; the lengths of a group add up to 8192 and the largest is exactly 2048. `prompt_of`: every prompt is extended by exactly 4 rollouts.
All inputs are finite; a program needn't handle non-finite values.
Results may differ from a plain program's by a relative error of at most 0.009.
The roundings to bfloat16 on the way count: a program that leaves them out, or rounds other values in their place, can miss the bound.
Values may be sent and summed in bfloat16 or wider, within the bound.
No kernel may reach another device: no remote copies, remote signals or barrier semaphores. Data moves between devices by JAX's collectives and lax.ppermute only.
A program may use at most 128 MiB of HBM per device.

v0:
```python
import functools
import math

import jax
import jax.numpy as jnp
from jax import lax
from jax.experimental import pallas as pl
from jax.experimental.pallas import tpu as pltpu
from jax.sharding import PartitionSpec as P


HD = 128
GUESS = 8


ROPE_BASE = 1000000.0
NEG_FILL = -1e30


def rotate(values, positions):
    half = values.shape[-1] // 2
    steps = jnp.arange(half).astype(jnp.float32) * (2.0 / values.shape[-1])
    freqs = jnp.exp(-math.log(ROPE_BASE) * steps)
    angles = positions[:, None] * freqs[None, :]
    cosine = jnp.cos(angles)[:, None, :]
    sine = jnp.sin(angles)[:, None, :]
    first = values[..., :half]
    second = values[..., half:]
    return jnp.concatenate(
        [first * cosine - second * sine, second * cosine + first * sine], axis=-1
    )


def lookup(table, indices):
    hits = indices[:, None] == jnp.arange(table.shape[0], dtype=jnp.int32)[None, :]
    return jnp.sum(jnp.where(hits, table[None, :], 0), axis=1)


def combine(first, second):
    peak_a, total_a, numer_a = first
    peak_b, total_b, numer_b = second
    peak = jnp.maximum(peak_a, peak_b)
    factor_a = jnp.exp(peak_a - peak)
    factor_b = jnp.exp(peak_b - peak)
    return (
        peak,
        total_a * factor_a + total_b * factor_b,
        numer_a * factor_a[..., None] + numer_b * factor_b[..., None],
    )


def masked_stats(scores, visible, values):
    peak = jnp.max(jnp.where(visible, scores, NEG_FILL), axis=-1)
    weights = jnp.exp(jnp.where(visible, scores - peak[..., None], NEG_FILL))
    total = jnp.sum(weights, axis=-1)
    numer = jnp.einsum(
        "rtkgs,rskd->rtkgd",
        weights.astype(jnp.bfloat16),
        values,
        preferred_element_type=jnp.float32,
    )
    return (peak, total, numer)


def general_body(
    hidden,
    w_query,
    w_key,
    w_value,
    b_query,
    b_key,
    b_value,
    w_out,
    prefix_keys,
    prefix_values,
    suffix_keys,
    suffix_values,
    suffix_lengths,
    prompt_of,
):
    row_count = hidden.shape[0]
    q_heads = w_query.shape[1] // HD
    kv_heads = w_key.shape[1] // HD
    group = q_heads // kv_heads
    prompts = prefix_keys.shape[0]
    pre_dev = prefix_keys.shape[1]
    prefix_total = pre_dev * lax.axis_size(("roll", "seq"))
    per_device = suffix_keys.shape[0]
    suf_dev = suffix_keys.shape[1]
    scale = 1.0 / math.sqrt(HD)
    q_part = jnp.dot(hidden, w_query, preferred_element_type=jnp.float32)
    k_part = jnp.dot(hidden, w_key, preferred_element_type=jnp.float32)
    v_part = jnp.dot(hidden, w_value, preferred_element_type=jnp.float32)
    q_sum, k_sum, v_sum = lax.psum((q_part, k_part, v_part), ("roll", "seq"))
    count = q_sum.shape[0]
    row_ids = jnp.arange(count, dtype=jnp.int32)
    owner_ids = row_ids // GUESS
    positions = (prefix_total + lookup(suffix_lengths, owner_ids) + row_ids % GUESS).astype(
        jnp.float32
    )
    q_rot = rotate((q_sum + b_query.astype(jnp.float32)).reshape(count, q_heads, HD), positions)
    k_rot = rotate((k_sum + b_key.astype(jnp.float32)).reshape(count, kv_heads, HD), positions)
    v_fin = (v_sum + b_value.astype(jnp.float32)).reshape(count, kv_heads, HD)
    query = q_rot.astype(jnp.bfloat16)
    key_new = k_rot.astype(jnp.bfloat16)
    value_new = v_fin.astype(jnp.bfloat16)
    query_grid = query.reshape(row_count, kv_heads, group, HD)
    owners_all = jnp.arange(row_count, dtype=jnp.int32) // GUESS
    row_prompt = lookup(prompt_of, owners_all)
    pre_keys = prefix_keys.reshape(prompts, pre_dev, kv_heads, HD)
    pre_values = prefix_values.reshape(prompts, pre_dev, kv_heads, HD)
    peak_all = jnp.full((row_count, kv_heads, group), NEG_FILL, jnp.float32)
    total_all = jnp.zeros((row_count, kv_heads, group), jnp.float32)
    numer_all = jnp.zeros((row_count, kv_heads, group, HD), jnp.float32)
    for prompt in range(prompts):
        scores = (
            jnp.einsum(
                "tkgd,skd->tkgs", query_grid, pre_keys[prompt], preferred_element_type=jnp.float32
            )
            * scale
        )
        block_peak = jnp.max(scores, axis=-1)
        weights = jnp.exp(scores - block_peak[..., None])
        block_numer = jnp.einsum(
            "tkgs,skd->tkgd",
            weights.astype(jnp.bfloat16),
            pre_values[prompt],
            preferred_element_type=jnp.float32,
        )
        picked = (row_prompt == prompt)[:, None, None]
        peak_all = jnp.where(picked, block_peak, peak_all)
        total_all = jnp.where(picked, jnp.sum(weights, axis=-1), total_all)
        numer_all = jnp.where(picked[..., None], block_numer, numer_all)
    first_rollout = lax.axis_index("roll") * per_device
    seq_index = lax.axis_index("seq")
    local_len = lax.dynamic_slice_in_dim(suffix_lengths, first_rollout, per_device, 0)
    live = jnp.clip(local_len - seq_index * suf_dev, 0, suf_dev)
    row_start = first_rollout * GUESS
    local_rows = per_device * GUESS
    query_local = lax.dynamic_slice_in_dim(query_grid, row_start, local_rows, 0).reshape(
        per_device, GUESS, kv_heads, group, HD
    )
    suf_keys = suffix_keys.reshape(per_device, suf_dev, kv_heads, HD)
    suf_values = suffix_values.reshape(per_device, suf_dev, kv_heads, HD)
    scores = (
        jnp.einsum("rtkgd,rskd->rtkgs", query_local, suf_keys, preferred_element_type=jnp.float32)
        * scale
    )
    visible = (jnp.arange(suf_dev, dtype=jnp.int32)[None, :] < live[:, None])[
        :, None, None, None, :
    ]
    suffix_part = masked_stats(scores, visible, suf_values)
    key_local = lax.dynamic_slice_in_dim(key_new, row_start, local_rows, 0).reshape(
        per_device, GUESS, kv_heads, HD
    )
    value_local = lax.dynamic_slice_in_dim(value_new, row_start, local_rows, 0).reshape(
        per_device, GUESS, kv_heads, HD
    )
    new_scores = (
        jnp.einsum("rtkgd,rskd->rtkgs", query_local, key_local, preferred_element_type=jnp.float32)
        * scale
    )
    guess_ids = jnp.arange(GUESS, dtype=jnp.int32)
    causal = (guess_ids[None, :] <= guess_ids[:, None]) & (seq_index == 0)
    guess_part = masked_stats(new_scores, causal[None, :, None, None, :], value_local)
    prefix_local = (
        lax.dynamic_slice_in_dim(peak_all, row_start, local_rows, 0).reshape(
            per_device, GUESS, kv_heads, group
        ),
        lax.dynamic_slice_in_dim(total_all, row_start, local_rows, 0).reshape(
            per_device, GUESS, kv_heads, group
        ),
        lax.dynamic_slice_in_dim(numer_all, row_start, local_rows, 0).reshape(
            per_device, GUESS, kv_heads, group, HD
        ),
    )
    peak_loc, total_loc, numer_loc = combine(combine(prefix_local, suffix_part), guess_part)
    peak_all = lax.dynamic_update_slice_in_dim(
        peak_all, peak_loc.reshape(local_rows, kv_heads, group), row_start, 0
    )
    total_all = lax.dynamic_update_slice_in_dim(
        total_all, total_loc.reshape(local_rows, kv_heads, group), row_start, 0
    )
    numer_all = lax.dynamic_update_slice_in_dim(
        numer_all, numer_loc.reshape(local_rows, kv_heads, group, HD), row_start, 0
    )
    peaks, totals, numers = (
        lax.all_to_all(peak_all[None], ("roll", "seq"), split_axis=1, concat_axis=0, tiled=True),
        lax.all_to_all(total_all[None], ("roll", "seq"), split_axis=1, concat_axis=0, tiled=True),
        lax.all_to_all(numer_all[None], ("roll", "seq"), split_axis=1, concat_axis=0, tiled=True),
    )
    peak_top = jnp.max(peaks, axis=0)
    factors = jnp.exp(peaks - peak_top[None])
    share = (
        jnp.sum(numers * factors[..., None], axis=0) / jnp.sum(totals * factors, axis=0)[..., None]
    )
    share = share.astype(jnp.bfloat16).reshape(share.shape[0], q_heads * HD)
    attention = lax.all_gather(share, ("roll", "seq"), axis=0, tiled=True)
    summed = lax.psum_scatter(
        jnp.dot(attention, w_out, preferred_element_type=jnp.float32),
        "tp",
        scatter_dimension=0,
        tiled=True,
    )
    return summed.astype(jnp.bfloat16)


VMEM_MOST = 66900000


def contract_last(a, b):
    return lax.dot_general(a, b, (((1,), (1,)), ((), ())), preferred_element_type=jnp.float32)


def project_kernel(flip, x_ref, wq_ref, wk_ref, wv_ref, out_ref, x_all, wq, wk, wv, sems):
    zone = lax.axis_index("roll")
    seq = lax.axis_index("seq")
    half = 1 - seq if flip else seq
    roll, kh, block, width = out_ref.shape
    wide = width - 2 * HD
    chunks = wq.shape[0]
    span = wq.shape[2]

    fetch = pltpu.make_async_copy(x_ref, x_all, sems.at[chunks + 2])
    fetch.start()
    copies = []
    for c in range(chunks):
        at = pl.multiple_of(half * (kh * wide) + c * span, span)
        copies.append(pltpu.make_async_copy(wq_ref.at[:, pl.ds(at, span)], wq.at[c], sems.at[c]))
    at = pl.multiple_of(half * (kh * HD), kh * HD)
    copies.append(pltpu.make_async_copy(wk_ref.at[:, pl.ds(at, kh * HD)], wk, sems.at[chunks]))
    copies.append(pltpu.make_async_copy(wv_ref.at[:, pl.ds(at, kh * HD)], wv, sems.at[chunks + 1]))
    for copy in copies:
        copy.start()
    fetch.wait()
    x = x_all[...]

    def place(part, j, at):
        for b in range(roll):
            out_ref[b ^ zone, j, :, at : at + part.shape[1]] = part[b * block : (b + 1) * block]

    for c in range(chunks):
        copies[c].wait()
        part = jnp.dot(x, wq[c], preferred_element_type=jnp.float32)
        place(part, c * span // wide, c * span % wide)
    for copy, w, at in ((copies[chunks], wk, wide), (copies[chunks + 1], wv, wide + HD)):
        copy.wait()
        part = jnp.dot(x, w[...], preferred_element_type=jnp.float32)
        for j in range(kh):
            place(part[:, j * HD : (j + 1) * HD], j, at)


def project(hidden, w_query, w_key, w_value, roll, kh, flip):
    rows, depth = hidden.shape
    kv_heads = w_key.shape[1] // HD
    wide = w_query.shape[1] // kv_heads
    block = rows // roll
    width = wide + 2 * HD
    span = min(wide, 512)
    chunks = kh * wide // span
    hbm = pl.BlockSpec(memory_space=pltpu.HBM)
    vmem = pl.BlockSpec(memory_space=pltpu.VMEM)
    return pl.pallas_call(
        functools.partial(project_kernel, flip),
        out_shape=jax.ShapeDtypeStruct((roll, kh, block, width), jnp.float32),
        in_specs=[hbm] * 4,
        out_specs=vmem,
        scratch_shapes=[
            pltpu.VMEM((rows, depth), jnp.bfloat16),
            pltpu.VMEM((chunks, depth, span), jnp.bfloat16),
            pltpu.VMEM((depth, kh * HD), jnp.bfloat16),
            pltpu.VMEM((depth, kh * HD), jnp.bfloat16),
            pltpu.SemaphoreType.DMA((chunks + 3,)),
        ],
        compiler_params=pltpu.CompilerParams(vmem_limit_bytes=VMEM_MOST - 4 * rows * width * kh),
        cost_estimate=pl.CostEstimate(
            flops=2 * rows * depth * width * kh,
            bytes_accessed=2 * depth * width * kh + 4 * rows * width * kh,
            transcendentals=0,
        ),
        name="project_send" if flip else "project_keep",
    )(hidden, w_query, w_key, w_value)


def finish_kernel(group, per, meta, keep_ref, got_ref, *refs):
    others = refs[:-8]
    bq_ref, bk_ref, bv_ref, cos_ref, sin_ref, q_ref, k_ref, v_ref = refs[-8:]
    kh = keep_ref.shape[1]
    guess = cos_ref.shape[0] // per
    cosine = cos_ref[...]
    sine = sin_ref[...]

    def total(j, g):
        at = slice(g * HD, (g + 1) * HD)
        u = keep_ref[0, j, :, at] + got_ref[0, j, :, at]
        for o in others:
            u = u + o[j, :, at]
        if g < group:
            bias = bq_ref[:, (j * group + g) * HD : (j * group + g + 1) * HD]
        else:
            bias = (bk_ref if g == group else bv_ref)[:, j * HD : (j + 1) * HD]
        return u + bias.astype(jnp.float32)

    def turn(u):
        return u * cosine + pltpu.roll(u, HD // 2, 1) * sine

    for j in range(kh):
        for g in range(0, group, 2):
            one = turn(total(j, g))
            two = turn(total(j, g + 1))
            for i in range(per):
                span = slice(i * guess, (i + 1) * guess)
                both = jnp.concatenate([one[span], two[span]], axis=0)
                q_ref[i, j, g * guess : (g + 2) * guess, :] = both.astype(jnp.bfloat16)
        k_ref[j] = turn(total(j, group)).astype(jnp.bfloat16)
        v_ref[j] = total(j, group + 1).astype(jnp.bfloat16)


def finish(meta, keep, got, others, biases, cosine, sine, per):
    _, kh, block, width = keep.shape
    group = width // HD - 2
    guess = block // per
    first = pl.BlockSpec((1, kh, block, width), lambda n, meta: (0, 0, 0, 0))
    part = pl.BlockSpec((kh, block, width), lambda n, meta: (0, 0, 0))
    table = pl.BlockSpec((block, HD), lambda n, meta: (meta[0], 0))

    def half(bias):
        return pl.BlockSpec((1, bias.shape[1] // 2), lambda n, meta: (0, meta[1]))

    return pl.pallas_call(
        functools.partial(finish_kernel, group, per),
        grid_spec=pltpu.PrefetchScalarGridSpec(
            num_scalar_prefetch=1,
            grid=(1,),
            in_specs=[first, first] + [part] * len(others) + [half(b) for b in biases] + [table, table],
            out_specs=(
                pl.BlockSpec((per, kh, group * guess, HD), lambda n, meta: (0, 0, 0, 0)),
                pl.BlockSpec((kh, block, HD), lambda n, meta: (0, 0, 0)),
                pl.BlockSpec((kh, block, HD), lambda n, meta: (0, 0, 0)),
            ),
        ),
        out_shape=(
            jax.ShapeDtypeStruct((per, kh, group * guess, HD), jnp.bfloat16),
            jax.ShapeDtypeStruct((kh, block, HD), jnp.bfloat16),
            jax.ShapeDtypeStruct((kh, block, HD), jnp.bfloat16),
        ),
        compiler_params=pltpu.CompilerParams(vmem_limit_bytes=16 << 20),
        name="finish",
    )(meta, keep, got, *others, *biases, cosine, sine)


def own_kernel(scale, guess, meta, lengths, q_ref, kn_ref, vn_ref, k0_ref, k1_ref, v0_ref, v1_ref, n_ref, m_ref, l_ref):
    per, kh, width, _ = q_ref.shape
    span = k0_ref.shape[1]
    seq = meta[1]
    fresh = kn_ref.shape[1]
    key_id = lax.broadcasted_iota(jnp.int32, (width, span), 1)
    new_id = lax.broadcasted_iota(jnp.int32, (width, fresh), 1)
    row_id = lax.broadcasted_iota(jnp.int32, (width, fresh), 0) % guess
    for i in range(per):
        length = lengths[meta[0] * per + i]
        sees = (key_id < length - seq * span, key_id < length - (1 - seq) * span)
        causal = (new_id >= i * guess) & (new_id - i * guess <= row_id)
        sees = sees + (causal,)
        for j in range(kh):
            q = q_ref[i, j]
            at = slice(j * HD, (j + 1) * HD)
            keys = (k0_ref[i, :, at], k1_ref[i, :, at], kn_ref[j])
            values = (v0_ref[i, :, at], v1_ref[i, :, at], vn_ref[j])
            scores = [jnp.where(see, contract_last(q, k) * scale, NEG_FILL) for k, see in zip(keys, sees)]
            peak = jnp.max(scores[0], axis=1, keepdims=True)
            for s in scores[1:]:
                peak = jnp.maximum(peak, jnp.max(s, axis=1, keepdims=True))
            total = jnp.zeros((width, 1), jnp.float32)
            numer = jnp.zeros((width, HD), jnp.float32)
            for s, v in zip(scores, values):
                w = jnp.exp(s - peak)
                total = total + jnp.sum(w, axis=1, keepdims=True)
                numer = numer + jnp.dot(w.astype(jnp.bfloat16), v, preferred_element_type=jnp.float32)
            n_ref[i, j] = numer
            m_ref[i, j] = jnp.broadcast_to(peak, (width, HD))
            l_ref[i, j] = jnp.broadcast_to(total, (width, HD))


def own_attention(meta, lengths, q, k_new, v_new, keys, keys_got, values, values_got, scale, guess):
    per, kh, width, _ = q.shape
    span = keys.shape[1]
    cols = kh * HD
    local = pl.BlockSpec((per, span, cols), lambda n, meta, lengths: (0, 0, meta[1]))
    got = pl.BlockSpec((per, span, cols), lambda n, meta, lengths: (0, 0, 0))
    fresh = pl.BlockSpec(k_new.shape, lambda n, meta, lengths: (0, 0, 0))
    whole = pl.BlockSpec(q.shape, lambda n, meta, lengths: (0, 0, 0, 0))
    out = jax.ShapeDtypeStruct(q.shape, jnp.float32)
    elements = per * kh * width * span * 2
    return pl.pallas_call(
        functools.partial(own_kernel, scale, guess),
        grid_spec=pltpu.PrefetchScalarGridSpec(
            num_scalar_prefetch=2,
            grid=(1,),
            in_specs=[whole, fresh, fresh, local, got, local, got],
            out_specs=(whole, whole, whole),
        ),
        out_shape=(out, out, out),
        compiler_params=pltpu.CompilerParams(vmem_limit_bytes=24 << 20),
        cost_estimate=pl.CostEstimate(
            flops=4 * elements * HD, bytes_accessed=8 * per * span * cols, transcendentals=elements
        ),
        name="own_attention",
    )(meta, lengths, q, k_new, v_new, keys, keys_got, values, values_got)


def split_three(x):
    high = x.astype(jnp.bfloat16).astype(jnp.float32)
    rest = x - high
    middle = rest.astype(jnp.bfloat16).astype(jnp.float32)
    return high, middle, rest - middle


def prefix_kernel(scale, roll, meta, prompts, *refs):
    q_refs = refs[:roll]
    k0_ref, k1_ref, v0_ref, v1_ref, on_ref, om_ref, ol_ref = refs[roll : roll + 7]
    n_out, m_out, l_out = refs[roll + 7 : roll + 10]
    packed = refs[roll + 10 : 2 * roll + 9]
    q_all, n_all, m_all, l_all, order = refs[2 * roll + 9 :]
    per, kh, width, _ = q_refs[0].shape
    prompt = pl.program_id(0)
    j = pl.program_id(1)
    share = roll * per // pl.num_programs(0)

    @pl.when((prompt == 0) & (j == 0))
    def _():
        for k in range(roll):
            q_all[k * per : (k + 1) * per] = q_refs[k][...]

    @pl.when(j == 0)
    def _():
        filled = jnp.int32(0)
        for k in range(roll):
            for i in range(per):
                chosen = prompts[(meta[0] ^ k) * per + i] == prompt

                @pl.when(chosen)
                def _():
                    order[filled] = k * per + i

                filled = filled + chosen.astype(jnp.int32)

    ids = [order[n] for n in range(share)]
    q = jnp.concatenate([q_all[at, j] for at in ids], axis=0)
    scores = [contract_last(q, k_ref[0]) * scale for k_ref in (k0_ref, k1_ref)]
    peak = jnp.maximum(
        jnp.max(scores[0], axis=1, keepdims=True), jnp.max(scores[1], axis=1, keepdims=True)
    )
    total = jnp.zeros(peak.shape, jnp.float32)
    numer = jnp.zeros((share * width, HD), jnp.float32)
    for s, v_ref in zip(scores, (v0_ref, v1_ref)):
        w = jnp.exp(s - peak)
        total = total + jnp.sum(w, axis=1, keepdims=True)
        numer = numer + jnp.dot(w.astype(jnp.bfloat16), v_ref[0], preferred_element_type=jnp.float32)
    peak = jnp.broadcast_to(peak, numer.shape)
    total = jnp.broadcast_to(total, numer.shape)
    for n, at in enumerate(ids):
        span = slice(n * width, (n + 1) * width)
        n_all[at, j] = numer[span]
        m_all[at, j] = peak[span]
        l_all[at, j] = total[span]

    @pl.when((prompt == pl.num_programs(0) - 1) & (j == kh - 1))
    def _():
        for i in range(per):
            for h in range(kh):
                m_a, m_b = m_all[i, h], om_ref[i, h]
                peak = jnp.maximum(m_a, m_b)
                f_a, f_b = jnp.exp(m_a - peak), jnp.exp(m_b - peak)
                m_out[i, h] = peak
                l_out[i, h] = l_all[i, h] * f_a + ol_ref[i, h] * f_b
                n_out[i, h] = n_all[i, h] * f_a + on_ref[i, h] * f_b
        lane = lax.broadcasted_iota(jnp.int32, (width, HD), 1)
        for k in range(1, roll):
            stats = jnp.zeros((width, HD), jnp.float32)
            for i in range(per):
                for h in range(kh):
                    u = i * kh + h
                    packed[k - 1][u * width : (u + 1) * width, :] = n_all[k * per + i, h].astype(jnp.bfloat16)
                    pieces = split_three(m_all[k * per + i, h]) + split_three(l_all[k * per + i, h])
                    for c, piece in enumerate(pieces):
                        stats = jnp.where(lane == 6 * u + c, piece, stats)
            u = per * kh
            packed[k - 1][u * width : (u + 1) * width, :] = stats.astype(jnp.bfloat16)


def prefix_attention(meta, prompt_of, queries, keys, keys_got, values, values_got, own, scale):
    roll = len(queries)
    per, kh, width, _ = queries[0].shape
    prompts, span, _ = keys.shape
    local = pl.BlockSpec((1, span, HD), lambda p, j, meta, prompts: (p, 0, meta[1] * kh + j))
    got = pl.BlockSpec((1, span, HD), lambda p, j, meta, prompts: (p, 0, j))
    whole = pl.BlockSpec(queries[0].shape, lambda p, j, meta, prompts: (0, 0, 0, 0))
    rows = (per * kh + 1) * width
    sent = pl.BlockSpec((rows, HD), lambda p, j, meta, prompts: (0, 0))
    out = jax.ShapeDtypeStruct(queries[0].shape, jnp.float32)
    elements = roll * per * kh * width * span * 2
    everything = (roll * per, kh, width, HD)
    outs = pl.pallas_call(
        functools.partial(prefix_kernel, scale, roll),
        grid_spec=pltpu.PrefetchScalarGridSpec(
            num_scalar_prefetch=2,
            grid=(prompts, kh),
            in_specs=[whole] * roll + [local, got, local, got] + [whole] * 3,
            out_specs=[whole] * 3 + [sent] * (roll - 1),
            scratch_shapes=[pltpu.VMEM(everything, jnp.bfloat16)] + [pltpu.VMEM(everything, jnp.float32)] * 3
            + [pltpu.SMEM((roll * per,), jnp.int32)],
        ),
        out_shape=[out] * 3 + [jax.ShapeDtypeStruct((rows, HD), jnp.bfloat16)] * (roll - 1),
        compiler_params=pltpu.CompilerParams(vmem_limit_bytes=24 << 20),
        cost_estimate=pl.CostEstimate(
            flops=4 * elements * HD, bytes_accessed=8 * prompts * span * kh * HD, transcendentals=elements
        ),
        name="prefix_attention",
    )(meta, prompt_of, *queries, keys, keys_got, values, values_got, *own)
    return outs[:3], outs[3:]


def merge_kernel(group, n_ref, m_ref, l_ref, *refs):
    packed, out_ref = refs[:-1], refs[-1]
    per, kh, width, _ = n_ref.shape
    guess = width // group
    stats = [p[per * kh * width :, :].astype(jnp.float32) for p in packed]
    results = {}
    for i in range(per):
        for h in range(kh):
            u = i * kh + h

            def column(s, c):
                c = 6 * u + c
                return s[:, c : c + 1] + s[:, c + 1 : c + 2] + s[:, c + 2 : c + 3]

            peaks = [m_ref[i, h]] + [jnp.broadcast_to(column(s, 0), (width, HD)) for s in stats]
            totals = [l_ref[i, h]] + [jnp.broadcast_to(column(s, 3), (width, HD)) for s in stats]
            numers = [n_ref[i, h]] + [p[u * width : (u + 1) * width, :].astype(jnp.float32) for p in packed]
            top = functools.reduce(jnp.maximum, peaks)
            total = jnp.zeros((width, HD), jnp.float32)
            numer = jnp.zeros((width, HD), jnp.float32)
            for m, l, n in zip(peaks, totals, numers):
                f = jnp.exp(m - top)
                total = total + l * f
                numer = numer + n * f
            results[i, h] = numer / total
    for h in range(kh):
        for g in range(group):
            rows = [results[i, h][g * guess : (g + 1) * guess] for i in range(per)]
            at = (h * group + g) * HD
            out_ref[:, at : at + HD] = jnp.concatenate(rows, axis=0).astype(jnp.bfloat16)


def merge(own, packed, group):
    per, kh, width, _ = own[0].shape
    whole = pl.BlockSpec(own[0].shape, lambda n: (0, 0, 0, 0))
    sent = pl.BlockSpec(packed[0].shape, lambda n: (0, 0))
    shape = (per * width // group, kh * group * HD)
    return pl.pallas_call(
        functools.partial(merge_kernel, group),
        grid=(1,),
        out_shape=jax.ShapeDtypeStruct(shape, jnp.bfloat16),
        in_specs=[whole] * 3 + [sent] * len(packed),
        out_specs=pl.BlockSpec(shape, lambda n: (0, 0)),
        compiler_params=pltpu.CompilerParams(vmem_limit_bytes=16 << 20),
        name="merge",
    )(*own, *packed)


def output_kernel(roll, *refs):
    parts = (refs[:roll], refs[roll : 2 * roll])
    w_ref, keep_ref, send_ref, w, lhs, sems = refs[2 * roll :]
    zone, seq, tp = lax.axis_index("roll"), lax.axis_index("seq"), lax.axis_index("tp")
    block, cols = parts[0][0].shape
    chunks, depth, _ = w.shape
    each = chunks // 2
    copies = []
    for c in range(chunks):
        side = seq if c < each else 1 - seq
        at = pl.multiple_of(side * cols + (c % each) * depth, depth)
        copies.append(pltpu.make_async_copy(w_ref.at[pl.ds(at, depth), :], w.at[c], sems.at[c]))
    for copy in copies:
        copy.start()
    for h in range(2):
        for k in range(roll):
            at = pl.multiple_of((zone ^ k ^ (tp * (roll // 2))) * block, block)
            lhs[h, pl.ds(at, block), :] = parts[h][k][...]
    total = None
    for c in range(chunks):
        copies[c].wait()
        at = (c % each) * depth
        part = jnp.dot(lhs[c // each, :, at : at + depth], w[c], preferred_element_type=jnp.float32)
        total = part if c == 0 else total + part
    rows = keep_ref.shape[0]
    keep_ref[...] = total[:rows]
    send_ref[...] = total[rows:].astype(send_ref.dtype)


def output(mine, theirs, w_out):
    roll = len(mine)
    block, cols = mine[0].shape
    depth = 512 if cols % 512 == 0 else cols
    chunks = 2 * cols // depth
    width = w_out.shape[1]
    rows = roll * block
    vmem = pl.BlockSpec(memory_space=pltpu.VMEM)
    return pl.pallas_call(
        functools.partial(output_kernel, roll),
        in_specs=[vmem] * (2 * roll) + [pl.BlockSpec(memory_space=pltpu.HBM)],
        out_specs=(vmem, vmem),
        scratch_shapes=[
            pltpu.VMEM((chunks, depth, width), jnp.bfloat16),
            pltpu.VMEM((2, rows, cols), jnp.bfloat16),
            pltpu.SemaphoreType.DMA((chunks,)),
        ],
        out_shape=(
            jax.ShapeDtypeStruct((rows // 2, width), jnp.float32),
            jax.ShapeDtypeStruct((rows // 2, width), jnp.bfloat16),
        ),
        compiler_params=pltpu.CompilerParams(vmem_limit_bytes=24 << 20),
        cost_estimate=pl.CostEstimate(
            flops=4 * rows * cols * width, bytes_accessed=4 * cols * width, transcendentals=0
        ),
        name="output",
    )(*mine, *theirs, w_out)


def fast_body(
    hidden,
    w_query,
    w_key,
    w_value,
    b_query,
    b_key,
    b_value,
    w_out,
    prefix_keys,
    prefix_values,
    suffix_keys,
    suffix_values,
    suffix_lengths,
    prompt_of,
):
    roll = lax.axis_size("roll")
    kv_heads = w_key.shape[1] // HD
    group = w_query.shape[1] // w_key.shape[1]
    kh = kv_heads // 2
    per = suffix_keys.shape[0]
    block = hidden.shape[0] // roll
    guess = block // per
    scale = 1.0 / math.sqrt(HD)
    zone = lax.axis_index("roll").astype(jnp.int32)
    seq = lax.axis_index("seq").astype(jnp.int32)
    tp = lax.axis_index("tp").astype(jnp.int32)

    def across(x):
        return lax.ppermute(x, "seq", [(0, 1), (1, 0)])

    def hop(x, k):
        return lax.ppermute(x, "roll", [(n, n ^ k) for n in range(roll)])

    def hops(pick):
        sent = {k: hop(pick(k), k) for k in reversed(range(1, roll))}
        return [sent[k] for k in range(1, roll)]

    send = project(hidden, w_query, w_key, w_value, roll, kh, True)
    got = across(send)
    keep = project(hidden, w_query, w_key, w_value, roll, kh, False)
    terms = tuple(keep[k] + got[k] for k in range(1, roll))
    caches = (suffix_keys, suffix_values, prefix_keys, prefix_values)
    terms, small = lax.optimization_barrier((terms, (suffix_lengths, b_query, b_key, b_value, zone, seq, *caches)))
    meta = jnp.stack(small[4:6])
    sums = hops(lambda k: terms[k - 1])
    caches = small[6:]

    def other_half(x):
        return across(lax.dynamic_slice_in_dim(x, (1 - seq) * (kh * HD), kh * HD, x.ndim - 1))

    sk_got, sv_got, pk_got, pv_got = [other_half(x) for x in caches]

    row_ids = jnp.arange(hidden.shape[0], dtype=jnp.int32)
    prefix_total = prefix_keys.shape[1] * roll * 2
    positions = (prefix_total + lookup(small[0], row_ids // guess) + row_ids % guess).astype(jnp.float32)
    half = HD // 2
    steps = jnp.arange(half).astype(jnp.float32) * (2.0 / HD)
    freqs = jnp.exp(-math.log(ROPE_BASE) * steps)
    angles = positions[:, None] * freqs[None, :]
    cosine = jnp.cos(angles)
    sine = jnp.sin(angles)
    cosine = jnp.concatenate([cosine, cosine], axis=-1)
    sine = jnp.concatenate([-sine, sine], axis=-1)
    biases = [b[None, :] for b in small[1:4]]

    q, k_new, v_new = finish(meta, keep, got, sums, biases, cosine, sine, per)
    queries = [q] + hops(lambda k: q)
    own = own_attention(
        meta, suffix_lengths, q, k_new, v_new, suffix_keys, sk_got, suffix_values, sv_got, scale, guess
    )
    own, packed = prefix_attention(
        meta, prompt_of, queries, prefix_keys, pk_got, prefix_values, pv_got, own, scale
    )
    packed = hops(lambda k: packed[k - 1])
    share = merge(own, packed, group)
    mine = [share] + hops(lambda k: share)
    theirs = [across(m) for m in mine]
    kept, sent = output(mine, theirs, w_out)
    arrived = lax.ppermute(sent, "tp", [(0, 1), (1, 0)])
    return (kept + arrived.astype(jnp.float32)).astype(jnp.bfloat16)


def body(*arrays):
    hidden, w_key, prompt_of, suffix_keys = arrays[0], arrays[2], arrays[13], arrays[10]
    roll = lax.axis_size("roll")
    block = hidden.shape[0] // roll
    fits = (
        lax.axis_size("seq") == 2
        and lax.axis_size("tp") == 2
        and roll & (roll - 1) == 0
        and (w_key.shape[1] // HD) % 2 == 0
        and block % 16 == 0
        and block == suffix_keys.shape[0] * GUESS
        and 6 * suffix_keys.shape[0] * (w_key.shape[1] // HD) <= 2 * HD
        and prompt_of.shape[0] % arrays[8].shape[0] == 0
    )
    if not fits:
        return general_body(*arrays)
    return fast_body(*arrays)


def solution(mesh):
    return jax.shard_map(
        body,
        mesh=mesh,
        in_specs=(
            P("groups", ("roll", "seq")),
            P(("roll", "seq"), "tp"),
            P(("roll", "seq"), "tp"),
            P(("roll", "seq"), "tp"),
            P("tp"),
            P("tp"),
            P("tp"),
            P("tp", ("roll", "seq")),
            P("groups", ("roll", "seq"), "tp"),
            P("groups", ("roll", "seq"), "tp"),
            P(("groups", "roll"), "seq", "tp"),
            P(("groups", "roll"), "seq", "tp"),
            P("groups"),
            P("groups"),
        ),
        out_specs=P(("groups", "tp"), ("roll", "seq")),
        check_vma=False,
    )
```

profile of v0, /device:TPU:0, one launch (start us, length us, event | category | flops | bytes accessed | tf_op | source)
XLA Modules:
  0.0 79.6 jit_solution(15627448756276989327)
XLA Ops:
  0.0 4.0 %project_send.1 = f32[4,2,16,1280]{3,2,1,0:T(8,128)} custom-call(bf16[64,1024]{1,0:T(8,128)(2,1)} %x_ref.3, bf16[1024,4096]{1,0:T(8,128)(2,1)} %wq_ref.3, bf16[1024,512]{1,0:T(8,128)(2,1)} %wk_ref.3, bf16[1024,512]{1,0:T(8,128)(2,1)} %wv_ref.3), custom_call_target="tpu_custom_call" | custom-call | flops 335544320 | bytes 5898240 | tf_op jit(solution)/shard_map/project_send/pallas_call | solution.py:263
  4.1 0.6 collective-permute-start
  4.6 4.0 %project_keep.1.keep_ref = f32[4,2,16,1280]{3,2,1,0:T(8,128)} custom-call(bf16[64,1024]{1,0:T(8,128)(2,1)} %x_ref.3, bf16[1024,4096]{1,0:T(8,128)(2,1)} %wq_ref.3, bf16[1024,512]{1,0:T(8,128)(2,1)} %wk_ref.3, bf16[1024,512]{1,0:T(8,128)(2,1)} %wv_ref.3), custom_call_target="tpu_custom_call" | custom-call | flops 335544320 | bytes 5898240 | tf_op jit(solution)/shard_map/project_keep/pallas_call | solution.py:263
  8.7 0.0 copy-start.1
  8.7 1.3 %fusion = (f32[2,16,1280]{2,1,0:T(8,128)S(1)}, f32[2,16,1280]{2,1,0:T(8,128)S(1)}, f32[2,16,1280]{2,1,0:T(8,128)S(1)}) fusion(f32[4,2,16,1280]{3,2,1,0:T(8,128)S(1)} %collective-permute-done.got_ref, f32[4,2,16,1280]{3,2,1,0:T(8,128)} %project_keep.1.keep_ref), kind=kLoop, calls=%fused_computation.1 | loop fusion | flops 122880 | bytes 1474560 | tf_op jit(solution)/shard_map/add | solution.py:671
  10.0 0.0 copy-start.3
  10.0 1.4 %constant_dynamic-slice_fusion = bf16[2,1024,256]{2,1,0:T(8,128)(2,1)S(1)} fusion(bf16[2,1024,512]{2,1,0:T(8,128)(2,1)} %v0_ref.1, s32[]{:T(128)S(6)} %select_n.33), kind=kLoop, calls=%fused_computation.16 | loop fusion | bytes 2097156 | tf_op jit(solution)/shard_map/dynamic_slice | solution.py:679
  11.4 0.1 collective-permute-start.10
  11.5 0.1 constant_dynamic-slice_fusion.1
  11.6 0.5 collective-permute-start.9
  12.2 2.7 %collective-permute-start.1 = (f32[2,16,1280]{2,1,0:T(8,128)S(1)}, f32[2,16,1280]{2,1,0:T(8,128)S(1)}, u32[]{:S(2)}, u32[]{:S(2)}) collective-permute-start(f32[2,16,1280]{2,1,0:T(8,128)S(1)} %get-tuple-element.34), channel_id=1, source_target_pairs={{0,4},{4,0},{8,12},{12,8},{1,5},{5,1},{9,13},{13,9},{2,6},{6,2},{1... | collective-permute-start | bytes 491528 | tf_op jit(solution)/shard_map/ppermute | solution.py:662
  14.9 0.2 collective-permute-start.7
  15.1 0.4 collective-permute-start.8
  15.6 0.1 select_reduce_fusion
  15.7 4.0 %collective-permute-done.1.refs_0_ = f32[2,16,1280]{2,1,0:T(8,128)S(1)} collective-permute-done((f32[2,16,1280]{2,1,0:T(8,128)S(1)}, f32[2,16,1280]{2,1,0:T(8,128)S(1)}, u32[]{:S(2)}, u32[]{:S(2)}) %collective-permute-start.1) | collective-permute-done | bytes 163872 | tf_op jit(solution)/shard_map/ppermute | solution.py:662
  19.6 2.8 %collective-permute-start.2 = (f32[2,16,1280]{2,1,0:T(8,128)S(1)}, f32[2,16,1280]{2,1,0:T(8,128)S(1)}, u32[]{:S(2)}, u32[]{:S(2)}) collective-permute-start(f32[2,16,1280]{2,1,0:T(8,128)S(1)} %get-tuple-element.35), channel_id=1, source_target_pairs={{0,8},{4,12},{8,0},{12,4},{1,9},{5,13},{9,1},{13,5},{2,10},{6,14},... | collective-permute-start | bytes 491528 | tf_op jit(solution)/shard_map/ppermute | solution.py:662
  22.4 0.2 fusion.3
  22.6 7.4 %collective-permute-done.2.refs_1_ = f32[2,16,1280]{2,1,0:T(8,128)S(1)} collective-permute-done((f32[2,16,1280]{2,1,0:T(8,128)S(1)}, f32[2,16,1280]{2,1,0:T(8,128)S(1)}, u32[]{:S(2)}, u32[]{:S(2)}) %collective-permute-start.2) | collective-permute-done | bytes 163872 | tf_op jit(solution)/shard_map/ppermute | solution.py:662
  30.0 3.4 %collective-permute-start.3 = (f32[2,16,1280]{2,1,0:T(8,128)S(1)}, f32[2,16,1280]{2,1,0:T(8,128)S(1)}, u32[]{:S(2)}, u32[]{:S(2)}) collective-permute-start(f32[2,16,1280]{2,1,0:T(8,128)S(1)} %get-tuple-element.36), channel_id=1, source_target_pairs={{0,12},{4,8},{8,4},{12,0},{1,13},{5,9},{9,5},{13,1},{2,14},{6,10},... | collective-permute-start | bytes 491528 | tf_op jit(solution)/shard_map/ppermute | solution.py:662
  33.3 0.1 pad_add_fusion.meta
  33.5 0.1 pad_maximum_fusion
  33.6 4.3 %collective-permute-done.3.refs_2_ = f32[2,16,1280]{2,1,0:T(8,128)S(1)} collective-permute-done((f32[2,16,1280]{2,1,0:T(8,128)S(1)}, f32[2,16,1280]{2,1,0:T(8,128)S(1)}, u32[]{:S(2)}, u32[]{:S(2)}) %collective-permute-start.3) | collective-permute-done | bytes 163872 | tf_op jit(solution)/shard_map/ppermute | solution.py:662
  37.8 0.7 finish.1
  38.5 2.4 %collective-permute-start.4 = (bf16[2,2,64,128]{3,2,1,0:T(8,128)(2,1)S(1)}, bf16[2,2,64,128]{3,2,1,0:T(8,128)(2,1)S(1)}, u32[]{:S(2)}, u32[]{:S(2)}) collective-permute-start(bf16[2,2,64,128]{3,2,1,0:T(8,128)(2,1)S(1)} %get-tuple-element.41.q_ref.refs_0_), channel_id=1, source_target_pairs={{0,4},{4,0},{8,12},{12,8},{1,5},{5,1},{9,13},{13,9},{2,6},{6,2},{1... | collective-permute-start | bytes 196616 | tf_op jit(solution)/shard_map/ppermute | solution.py:662
  40.9 1.7 %collective-permute-start.5 = (bf16[2,2,64,128]{3,2,1,0:T(8,128)(2,1)S(1)}, bf16[2,2,64,128]{3,2,1,0:T(8,128)(2,1)S(1)}, u32[]{:S(2)}, u32[]{:S(2)}) collective-permute-start(bf16[2,2,64,128]{3,2,1,0:T(8,128)(2,1)S(1)} %get-tuple-element.41.q_ref.refs_0_), channel_id=1, source_target_pairs={{0,8},{4,12},{8,0},{12,4},{1,9},{5,13},{9,1},{13,5},{2,10},{6,14},... | collective-permute-start | bytes 196616 | tf_op jit(solution)/shard_map/ppermute | solution.py:662
  42.6 0.8 collective-permute-start.6
  43.4 2.6 %own_attention.1 = (f32[2,2,64,128]{3,2,1,0:T(8,128)S(1)}, f32[2,2,64,128]{3,2,1,0:T(8,128)S(1)}, f32[2,2,64,128]{3,2,1,0:T(8,128)S(1)}) custom-call(s32[2]{0:T(128)S(1)} %pad_add_fusion.meta, s32[8]{0:T(128)S(1)} %copy-done.6, bf16[2,2,64,128]{3,2,1,0:T(8,128)(2,1)S(1)} %get-tuple-element.41.q_ref.refs_0_, ...), custom_call_target="tpu_custom_call" | custom-call | flops 268435456 | bytes 4194304 | tf_op jit(solution)/shard_map/own_attention/pallas_call | solution.py:395
  46.0 1.3 %collective-permute-done.5.refs_2_ = bf16[2,2,64,128]{3,2,1,0:T(8,128)(2,1)S(1)} collective-permute-done((bf16[2,2,64,128]{3,2,1,0:T(8,128)(2,1)S(1)}, bf16[2,2,64,128]{3,2,1,0:T(8,128)(2,1)S(1)}, u32[]{:S(2)}, u32[]{:S(2)}) %collective-permute-start.5) | collective-permute-done | bytes 65568 | tf_op jit(solution)/shard_map/ppermute | solution.py:662
  47.3 1.4 %collective-permute-done.6.refs_3_ = bf16[2,2,64,128]{3,2,1,0:T(8,128)(2,1)S(1)} collective-permute-done((bf16[2,2,64,128]{3,2,1,0:T(8,128)(2,1)S(1)}, bf16[2,2,64,128]{3,2,1,0:T(8,128)(2,1)S(1)}, u32[]{:S(2)}, u32[]{:S(2)}) %collective-permute-start.6) | collective-permute-done | bytes 65568 | tf_op jit(solution)/shard_map/ppermute | solution.py:662
  48.7 4.2 %prefix_attention.1 = (f32[2,2,64,128]{3,2,1,0:T(8,128)S(1)}, f32[2,2,64,128]{3,2,1,0:T(8,128)S(1)}, f32[2,2,64,128]{3,2,1,0:T(8,128)S(1)}, bf16[320,128]{1,0:T(...) custom-call(s32[2]{0:T(128)S(1)} %pad_add_fusion.meta, s32[8]{0:T(128)S(1)} %copy-done.5, ...), custom_call_target="tpu_custom_call" | custom-call | flops 536870912 | bytes 2097152 | tf_op jit(solution)/shard_map/prefix_attention/pallas_call | solution.py:504
  52.9 0.1 collective-permute-start.11
  53.0 1.9 %collective-permute-start.12 = (bf16[320,128]{1,0:T(8,128)(2,1)S(1)}, bf16[320,128]{1,0:T(8,128)(2,1)S(1)}, u32[]{:S(2)}, u32[]{:S(2)}) collective-permute-start(bf16[320,128]{1,0:T(8,128)(2,1)S(1)} %get-tuple-element.55), channel_id=1, source_target_pairs={{0,8},{4,12},{8,0},{12,4},{1,9},{5,13},{9,1},{13,5},{2,10},{6,14},... | collective-permute-start | bytes 245768 | tf_op jit(solution)/shard_map/ppermute | solution.py:662
  54.9 2.5 %collective-permute-start.13 = (bf16[320,128]{1,0:T(8,128)(2,1)S(1)}, bf16[320,128]{1,0:T(8,128)(2,1)S(1)}, u32[]{:S(2)}, u32[]{:S(2)}) collective-permute-start(bf16[320,128]{1,0:T(8,128)(2,1)S(1)} %get-tuple-element.56), channel_id=1, source_target_pairs={{0,12},{4,8},{8,4},{12,0},{1,13},{5,9},{9,5},{13,1},{2,14},{6,10},... | collective-permute-start | bytes 245768 | tf_op jit(solution)/shard_map/ppermute | solution.py:662
  57.4 0.2 collective-permute-done.11.refs_0_
  57.6 3.7 %collective-permute-done.12.refs_1_ = bf16[320,128]{1,0:T(8,128)(2,1)S(1)} collective-permute-done((bf16[320,128]{1,0:T(8,128)(2,1)S(1)}, bf16[320,128]{1,0:T(8,128)(2,1)S(1)}, u32[]{:S(2)}, u32[]{:S(2)}) %collective-permute-start.12) | collective-permute-done | bytes 81952 | tf_op jit(solution)/shard_map/ppermute | solution.py:662
  61.3 0.4 merge.1.refs_0_
  61.7 1.5 %collective-permute-start.14 = (bf16[16,2048]{1,0:T(8,128)(2,1)S(1)}, bf16[16,2048]{1,0:T(8,128)(2,1)S(1)}, u32[]{:S(2)}, u32[]{:S(2)}) collective-permute-start(bf16[16,2048]{1,0:T(8,128)(2,1)S(1)} %merge.1.refs_0_), channel_id=1, source_target_pairs={{0,4},{4,0},{8,12},{12,8},{1,5},{5,1},{9,13},{13,9},{2,6},{6,2},{1... | collective-permute-start | bytes 196616 | tf_op jit(solution)/shard_map/ppermute | solution.py:662
  63.2 1.6 %collective-permute-start.15 = (bf16[16,2048]{1,0:T(8,128)(2,1)S(1)}, bf16[16,2048]{1,0:T(8,128)(2,1)S(1)}, u32[]{:S(2)}, u32[]{:S(2)}) collective-permute-start(bf16[16,2048]{1,0:T(8,128)(2,1)S(1)} %merge.1.refs_0_), channel_id=1, source_target_pairs={{0,8},{4,12},{8,0},{12,4},{1,9},{5,13},{9,1},{13,5},{2,10},{6,14},... | collective-permute-start | bytes 196616 | tf_op jit(solution)/shard_map/ppermute | solution.py:662
  64.8 1.4 %collective-permute-start.16 = (bf16[16,2048]{1,0:T(8,128)(2,1)S(1)}, bf16[16,2048]{1,0:T(8,128)(2,1)S(1)}, u32[]{:S(2)}, u32[]{:S(2)}) collective-permute-start(bf16[16,2048]{1,0:T(8,128)(2,1)S(1)} %merge.1.refs_0_), channel_id=1, source_target_pairs={{0,12},{4,8},{8,4},{12,0},{1,13},{5,9},{9,5},{13,1},{2,14},{6,10},... | collective-permute-start | bytes 196616 | tf_op jit(solution)/shard_map/ppermute | solution.py:662
  66.1 0.5 collective-permute-start.18
  66.7 3.1 %collective-permute-done.15.refs_2_ = bf16[16,2048]{1,0:T(8,128)(2,1)S(1)} collective-permute-done((bf16[16,2048]{1,0:T(8,128)(2,1)S(1)}, bf16[16,2048]{1,0:T(8,128)(2,1)S(1)}, u32[]{:S(2)}, u32[]{:S(2)}) %collective-permute-start.15) | collective-permute-done | bytes 65568 | tf_op jit(solution)/shard_map/ppermute | solution.py:662
  69.8 1.1 %collective-permute-done.16.refs_3_ = bf16[16,2048]{1,0:T(8,128)(2,1)S(1)} collective-permute-done((bf16[16,2048]{1,0:T(8,128)(2,1)S(1)}, bf16[16,2048]{1,0:T(8,128)(2,1)S(1)}, u32[]{:S(2)}, u32[]{:S(2)}) %collective-permute-start.16) | collective-permute-done | bytes 65568 | tf_op jit(solution)/shard_map/ppermute | solution.py:662
  70.9 0.1 collective-permute-done.19.refs_6_
  71.0 1.1 %collective-permute-done.20.refs_7_ = bf16[16,2048]{1,0:T(8,128)(2,1)S(1)} collective-permute-done((bf16[16,2048]{1,0:T(8,128)(2,1)S(1)}, bf16[16,2048]{1,0:T(8,128)(2,1)S(1)}, u32[]{:S(2)}, u32[]{:S(2)}) %collective-permute-start.20) | collective-permute-done | bytes 65568 | tf_op jit(solution)/shard_map/ppermute | solution.py:659
  72.2 2.4 %output.1 = (f32[32,1024]{1,0:T(8,128)S(1)}, bf16[32,1024]{1,0:T(8,128)(2,1)S(1)}) custom-call(bf16[16,2048]{1,0:T(8,128)(2,1)S(1)} %merge.1.refs_0_, bf16[16,2048]{1,0:T(8,128)(2,1)S(1)} %collective-permute-done.14.refs_1_, bf16[16,2048]{1,0:T(8,128)(2,1)S(1)} %collective-permute-done.15.refs_2_, bf16[16,2048]{1,0:T(8,128)(2,1)S(1)} %collective-permute-done.16.refs_3_, ...), custom_call_target="tpu_custom_call" | custom-call | flops 536870912 | bytes 8388608 | tf_op jit(solution)/shard_map/output/pallas_call | solution.py:609
  74.6 1.6 %collective-permute-start.21 = (bf16[32,1024]{1,0:T(8,128)(2,1)S(1)}, bf16[32,1024]{1,0:T(8,128)(2,1)S(1)}, u32[]{:S(2)}, u32[]{:S(2)}) collective-permute-start(bf16[32,1024]{1,0:T(8,128)(2,1)S(1)} %get-tuple-element.58), channel_id=1, source_target_pairs={{0,2},{2,0},{1,3},{3,1},{4,6},{6,4},{5,7},{7,5},{8,10},{10,8},{9,1... | collective-permute-start | bytes 196616 | tf_op jit(solution)/shard_map/ppermute | solution.py:709
  76.2 2.8 %collective-permute-done.21 = bf16[32,1024]{1,0:T(8,128)(2,1)S(1)} collective-permute-done((bf16[32,1024]{1,0:T(8,128)(2,1)S(1)}, bf16[32,1024]{1,0:T(8,128)(2,1)S(1)}, u32[]{:S(2)}, u32[]{:S(2)}) %collective-permute-start.21) | collective-permute-done | bytes 65568 | tf_op jit(solution)/shard_map/ppermute | solution.py:709
  78.9 0.6 add_convert_fusion
  (44 shorter events, 0.2 us)
Async XLA Ops:
  4.1 4.6 %collective-permute-start = (f32[4,2,16,1280]{3,2,1,0:T(8,128)}, f32[4,2,16,1280]{3,2,1,0:T(8,128)S(1)}, u32[]{:S(2)}, u32[]{:S(2)}) collective-permute-start(f32[4,2,16,1280]{3,2,1,0:T(8,128)} %project_send.1), channel_id=1, source_target_pairs={{0,1},{1,0},{2,3},{3,2},{4,5},{5,4},{6,7},{7,6},{8,9},{9,8},{10,11... | collective-permute-start | bytes 1966088 | tf_op jit(solution)/shard_map/ppermute | solution.py:659
  8.7 2.9 %copy-start.1 = (bf16[2,1024,512]{2,1,0:T(8,128)(2,1)S(1)}, bf16[2,1024,512]{2,1,0:T(8,128)(2,1)}, u32[]{:S(2)}) copy-start(bf16[2,1024,512]{2,1,0:T(8,128)(2,1)} %k0_ref.1) | copy-start | bytes 6291460
  10.0 4.9 %copy-start.3 = (bf16[2,512,512]{2,1,0:T(8,128)(2,1)S(1)}, bf16[2,512,512]{2,1,0:T(8,128)(2,1)}, u32[]{:S(2)}) copy-start(bf16[2,512,512]{2,1,0:T(8,128)(2,1)} %refs_4_.1) | copy-start | bytes 3145732
  11.4 3.7 %copy-start.4 = (bf16[2,512,512]{2,1,0:T(8,128)(2,1)S(1)}, bf16[2,512,512]{2,1,0:T(8,128)(2,1)}, u32[]{:S(2)}) copy-start(bf16[2,512,512]{2,1,0:T(8,128)(2,1)} %refs_6_.1) | copy-start | bytes 3145732
  11.4 4.2 %copy-start.6 = (s32[8]{0:T(128)S(1)}, s32[8]{0:T(128)}, u32[]{:S(2)}) copy-start(s32[8]{0:T(128)} %lengths.1) | copy-start | bytes 100
  11.4 22.0 %copy-start.7 = (bf16[4096]{0:T(1024)(128)(2,1)S(1)}, bf16[4096]{0:T(1024)(128)(2,1)}, u32[]{:S(2)}) copy-start(bf16[4096]{0:T(1024)(128)(2,1)} %param.18) | copy-start | bytes 24580
  11.4 22.0 %copy-start.8 = (bf16[512]{0:T(512)(128)(2,1)S(1)}, bf16[512]{0:T(512)(128)(2,1)}, u32[]{:S(2)}) copy-start(bf16[512]{0:T(512)(128)(2,1)} %param.19) | copy-start | bytes 3076
  11.4 22.0 %copy-start.9 = (bf16[512]{0:T(512)(128)(2,1)S(1)}, bf16[512]{0:T(512)(128)(2,1)}, u32[]{:S(2)}) copy-start(bf16[512]{0:T(512)(128)(2,1)} %param.20) | copy-start | bytes 3076
  11.4 26.4 %copy-start = (f32[4,2,16,1280]{3,2,1,0:T(8,128)S(1)}, f32[4,2,16,1280]{3,2,1,0:T(8,128)}, u32[]{:S(2)}) copy-start(f32[4,2,16,1280]{3,2,1,0:T(8,128)} %project_keep.1.keep_ref) | copy-start | bytes 1966084
  11.4 29.5 %collective-permute-start.10 = (bf16[2,1024,256]{2,1,0:T(8,128)(2,1)S(1)}, bf16[2,1024,256]{2,1,0:T(8,128)(2,1)S(1)}, u32[]{:S(2)}, u32[]{:S(2)}) collective-permute-start(bf16[2,1024,256]{2,1,0:T(8,128)(2,1)S(1)} %constant_dynamic-slice_fusion), channel_id=1, source_target_pairs={{0,1},{1,0},{2,3},{3,2},{4,5},{5,4},{6,7},{7,6},{8,9},{9,8},{10,11... | collective-permute-start | bytes 3145736 | tf_op jit(solution)/shard_map/ppermute | solution.py:659
  11.6 30.9 %collective-permute-start.9 = (bf16[2,1024,256]{2,1,0:T(8,128)(2,1)S(1)}, bf16[2,1024,256]{2,1,0:T(8,128)(2,1)S(1)}, u32[]{:S(2)}, u32[]{:S(2)}) collective-permute-start(bf16[2,1024,256]{2,1,0:T(8,128)(2,1)S(1)} %constant_dynamic-slice_fusion.1), channel_id=1, source_target_pairs={{0,1},{1,0},{2,3},{3,2},{4,5},{5,4},{6,7},{7,6},{8,9},{9,8},{10,11... | collective-permute-start | bytes 3145736 | tf_op jit(solution)/shard_map/ppermute | solution.py:659
  12.2 31.2 %copy-start.2 = (bf16[2,1024,512]{2,1,0:T(8,128)(2,1)S(1)}, bf16[2,1024,512]{2,1,0:T(8,128)(2,1)}, u32[]{:S(2)}) copy-start(bf16[2,1024,512]{2,1,0:T(8,128)(2,1)} %v0_ref.1) | copy-start | bytes 6291460
  12.2 7.4 %collective-permute-start.1 = (f32[2,16,1280]{2,1,0:T(8,128)S(1)}, f32[2,16,1280]{2,1,0:T(8,128)S(1)}, u32[]{:S(2)}, u32[]{:S(2)}) collective-permute-start(f32[2,16,1280]{2,1,0:T(8,128)S(1)} %get-tuple-element.34), channel_id=1, source_target_pairs={{0,4},{4,0},{8,12},{12,8},{1,5},{5,1},{9,13},{13,9},{2,6},{6,2},{1... | collective-permute-start | bytes 491528 | tf_op jit(solution)/shard_map/ppermute | solution.py:662
  14.8 57.3 %slice-start = ((s8[8388608]{0:T(1024)(128)(4,1)}), s8[4194304]{0:T(1024)(128)(4,1)S(1)}, s32[]{:S(2)}) async-start(s8[8388608]{0:T(1024)(128)(4,1)} %bitcast.8), calls=%async_computation | async-start | bytes 8388608
  14.9 33.8 %collective-permute-start.7 = (bf16[2,512,256]{2,1,0:T(8,128)(2,1)S(1)}, bf16[2,512,256]{2,1,0:T(8,128)(2,1)S(1)}, u32[]{:S(2)}, u32[]{:S(2)}) collective-permute-start(bf16[2,512,256]{2,1,0:T(8,128)(2,1)S(1)} %constant_dynamic-slice_fusion.3), channel_id=1, source_target_pairs={{0,1},{1,0},{2,3},{3,2},{4,5},{5,4},{6,7},{7,6},{8,9},{9,8},{10,11... | collective-permute-start | bytes 1572872 | tf_op jit(solution)/shard_map/ppermute | solution.py:659
  15.1 33.6 %collective-permute-start.8 = (bf16[2,512,256]{2,1,0:T(8,128)(2,1)S(1)}, bf16[2,512,256]{2,1,0:T(8,128)(2,1)S(1)}, u32[]{:S(2)}, u32[]{:S(2)}) collective-permute-start(bf16[2,512,256]{2,1,0:T(8,128)(2,1)S(1)} %constant_dynamic-slice_fusion.2), channel_id=1, source_target_pairs={{0,1},{1,0},{2,3},{3,2},{4,5},{5,4},{6,7},{7,6},{8,9},{9,8},{10,11... | collective-permute-start | bytes 1572872 | tf_op jit(solution)/shard_map/ppermute | solution.py:659
  19.6 10.4 %collective-permute-start.2 = (f32[2,16,1280]{2,1,0:T(8,128)S(1)}, f32[2,16,1280]{2,1,0:T(8,128)S(1)}, u32[]{:S(2)}, u32[]{:S(2)}) collective-permute-start(f32[2,16,1280]{2,1,0:T(8,128)S(1)} %get-tuple-element.35), channel_id=1, source_target_pairs={{0,8},{4,12},{8,0},{12,4},{1,9},{5,13},{9,1},{13,5},{2,10},{6,14},... | collective-permute-start | bytes 491528 | tf_op jit(solution)/shard_map/ppermute | solution.py:662
  30.0 7.9 %collective-permute-start.3 = (f32[2,16,1280]{2,1,0:T(8,128)S(1)}, f32[2,16,1280]{2,1,0:T(8,128)S(1)}, u32[]{:S(2)}, u32[]{:S(2)}) collective-permute-start(f32[2,16,1280]{2,1,0:T(8,128)S(1)} %get-tuple-element.36), channel_id=1, source_target_pairs={{0,12},{4,8},{8,4},{12,0},{1,13},{5,9},{9,5},{13,1},{2,14},{6,10},... | collective-permute-start | bytes 491528 | tf_op jit(solution)/shard_map/ppermute | solution.py:662
  38.5 7.5 %collective-permute-start.4 = (bf16[2,2,64,128]{3,2,1,0:T(8,128)(2,1)S(1)}, bf16[2,2,64,128]{3,2,1,0:T(8,128)(2,1)S(1)}, u32[]{:S(2)}, u32[]{:S(2)}) collective-permute-start(bf16[2,2,64,128]{3,2,1,0:T(8,128)(2,1)S(1)} %get-tuple-element.41.q_ref.refs_0_), channel_id=1, source_target_pairs={{0,4},{4,0},{8,12},{12,8},{1,5},{5,1},{9,13},{13,9},{2,6},{6,2},{1... | collective-permute-start | bytes 196616 | tf_op jit(solution)/shard_map/ppermute | solution.py:662
  40.9 6.4 %collective-permute-start.5 = (bf16[2,2,64,128]{3,2,1,0:T(8,128)(2,1)S(1)}, bf16[2,2,64,128]{3,2,1,0:T(8,128)(2,1)S(1)}, u32[]{:S(2)}, u32[]{:S(2)}) collective-permute-start(bf16[2,2,64,128]{3,2,1,0:T(8,128)(2,1)S(1)} %get-tuple-element.41.q_ref.refs_0_), channel_id=1, source_target_pairs={{0,8},{4,12},{8,0},{12,4},{1,9},{5,13},{9,1},{13,5},{2,10},{6,14},... | collective-permute-start | bytes 196616 | tf_op jit(solution)/shard_map/ppermute | solution.py:662
  42.6 6.1 %collective-permute-start.6 = (bf16[2,2,64,128]{3,2,1,0:T(8,128)(2,1)S(1)}, bf16[2,2,64,128]{3,2,1,0:T(8,128)(2,1)S(1)}, u32[]{:S(2)}, u32[]{:S(2)}) collective-permute-start(bf16[2,2,64,128]{3,2,1,0:T(8,128)(2,1)S(1)} %get-tuple-element.41.q_ref.refs_0_), channel_id=1, source_target_pairs={{0,12},{4,8},{8,4},{12,0},{1,13},{5,9},{9,5},{13,1},{2,14},{6,10},... | collective-permute-start | bytes 196616 | tf_op jit(solution)/shard_map/ppermute | solution.py:662
  43.4 5.4 %copy-start.5 = (s32[8]{0:T(128)S(1)}, s32[8]{0:T(128)}, u32[]{:S(2)}) copy-start(s32[8]{0:T(128)} %prompts.1) | copy-start | bytes 100
  43.4 28.8 %slice-start.1 = ((s8[8388608]{0:T(1024)(128)(4,1)}), s8[4194304]{0:T(1024)(128)(4,1)S(1)}, s32[]{:S(2)}) async-start(s8[8388608]{0:T(1024)(128)(4,1)} %bitcast.8), calls=%async_computation.1 | async-start | bytes 8388608
  52.9 4.6 %collective-permute-start.11 = (bf16[320,128]{1,0:T(8,128)(2,1)S(1)}, bf16[320,128]{1,0:T(8,128)(2,1)S(1)}, u32[]{:S(2)}, u32[]{:S(2)}) collective-permute-start(bf16[320,128]{1,0:T(8,128)(2,1)S(1)} %get-tuple-element.54), channel_id=1, source_target_pairs={{0,4},{4,0},{8,12},{12,8},{1,5},{5,1},{9,13},{13,9},{2,6},{6,2},{1... | collective-permute-start | bytes 245768 | tf_op jit(solution)/shard_map/ppermute | solution.py:662
  53.0 8.3 %collective-permute-start.12 = (bf16[320,128]{1,0:T(8,128)(2,1)S(1)}, bf16[320,128]{1,0:T(8,128)(2,1)S(1)}, u32[]{:S(2)}, u32[]{:S(2)}) collective-permute-start(bf16[320,128]{1,0:T(8,128)(2,1)S(1)} %get-tuple-element.55), channel_id=1, source_target_pairs={{0,8},{4,12},{8,0},{12,4},{1,9},{5,13},{9,1},{13,5},{2,10},{6,14},... | collective-permute-start | bytes 245768 | tf_op jit(solution)/shard_map/ppermute | solution.py:662
  54.9 6.4 %collective-permute-start.13 = (bf16[320,128]{1,0:T(8,128)(2,1)S(1)}, bf16[320,128]{1,0:T(8,128)(2,1)S(1)}, u32[]{:S(2)}, u32[]{:S(2)}) collective-permute-start(bf16[320,128]{1,0:T(8,128)(2,1)S(1)} %get-tuple-element.56), channel_id=1, source_target_pairs={{0,12},{4,8},{8,4},{12,0},{1,13},{5,9},{9,5},{13,1},{2,14},{6,10},... | collective-permute-start | bytes 245768 | tf_op jit(solution)/shard_map/ppermute | solution.py:662
  61.7 4.5 %collective-permute-start.14 = (bf16[16,2048]{1,0:T(8,128)(2,1)S(1)}, bf16[16,2048]{1,0:T(8,128)(2,1)S(1)}, u32[]{:S(2)}, u32[]{:S(2)}) collective-permute-start(bf16[16,2048]{1,0:T(8,128)(2,1)S(1)} %merge.1.refs_0_), channel_id=1, source_target_pairs={{0,4},{4,0},{8,12},{12,8},{1,5},{5,1},{9,13},{13,9},{2,6},{6,2},{1... | collective-permute-start | bytes 196616 | tf_op jit(solution)/shard_map/ppermute | solution.py:662
  63.2 6.6 %collective-permute-start.15 = (bf16[16,2048]{1,0:T(8,128)(2,1)S(1)}, bf16[16,2048]{1,0:T(8,128)(2,1)S(1)}, u32[]{:S(2)}, u32[]{:S(2)}) collective-permute-start(bf16[16,2048]{1,0:T(8,128)(2,1)S(1)} %merge.1.refs_0_), channel_id=1, source_target_pairs={{0,8},{4,12},{8,0},{12,4},{1,9},{5,13},{9,1},{13,5},{2,10},{6,14},... | collective-permute-start | bytes 196616 | tf_op jit(solution)/shard_map/ppermute | solution.py:662
  64.8 6.2 %collective-permute-start.16 = (bf16[16,2048]{1,0:T(8,128)(2,1)S(1)}, bf16[16,2048]{1,0:T(8,128)(2,1)S(1)}, u32[]{:S(2)}, u32[]{:S(2)}) collective-permute-start(bf16[16,2048]{1,0:T(8,128)(2,1)S(1)} %merge.1.refs_0_), channel_id=1, source_target_pairs={{0,12},{4,8},{8,4},{12,0},{1,13},{5,9},{9,5},{13,1},{2,14},{6,10},... | collective-permute-start | bytes 196616 | tf_op jit(solution)/shard_map/ppermute | solution.py:662
  66.1 4.8 %collective-permute-start.17 = (bf16[16,2048]{1,0:T(8,128)(2,1)S(1)}, bf16[16,2048]{1,0:T(8,128)(2,1)S(1)}, u32[]{:S(2)}, u32[]{:S(2)}) collective-permute-start(bf16[16,2048]{1,0:T(8,128)(2,1)S(1)} %merge.1.refs_0_), channel_id=1, source_target_pairs={{0,1},{1,0},{2,3},{3,2},{4,5},{5,4},{6,7},{7,6},{8,9},{9,8},{10,11... | collective-permute-start | bytes 196616 | tf_op jit(solution)/shard_map/ppermute | solution.py:659
  66.1 4.8 %collective-permute-start.18 = (bf16[16,2048]{1,0:T(8,128)(2,1)S(1)}, bf16[16,2048]{1,0:T(8,128)(2,1)S(1)}, u32[]{:S(2)}, u32[]{:S(2)}) collective-permute-start(bf16[16,2048]{1,0:T(8,128)(2,1)S(1)} %collective-permute-done.14.refs_1_), channel_id=1, source_target_pairs={{0,1},{1,0},{2,3},{3,2},{4,5},{5,4},{6,7},{7,6},{8,9},{9,8},{10,11... | collective-permute-start | bytes 196616 | tf_op jit(solution)/shard_map/ppermute | solution.py:659
  69.8 1.3 %collective-permute-start.19 = (bf16[16,2048]{1,0:T(8,128)(2,1)S(1)}, bf16[16,2048]{1,0:T(8,128)(2,1)S(1)}, u32[]{:S(2)}, u32[]{:S(2)}) collective-permute-start(bf16[16,2048]{1,0:T(8,128)(2,1)S(1)} %collective-permute-done.15.refs_2_), channel_id=1, source_target_pairs={{0,1},{1,0},{2,3},{3,2},{4,5},{5,4},{6,7},{7,6},{8,9},{9,8},{10,11... | collective-permute-start | bytes 196616 | tf_op jit(solution)/shard_map/ppermute | solution.py:659
  70.9 1.3 %collective-permute-start.20 = (bf16[16,2048]{1,0:T(8,128)(2,1)S(1)}, bf16[16,2048]{1,0:T(8,128)(2,1)S(1)}, u32[]{:S(2)}, u32[]{:S(2)}) collective-permute-start(bf16[16,2048]{1,0:T(8,128)(2,1)S(1)} %collective-permute-done.16.refs_3_), channel_id=1, source_target_pairs={{0,1},{1,0},{2,3},{3,2},{4,5},{5,4},{6,7},{7,6},{8,9},{9,8},{10,11... | collective-permute-start | bytes 196616 | tf_op jit(solution)/shard_map/ppermute | solution.py:659
  74.6 4.3 %collective-permute-start.21 = (bf16[32,1024]{1,0:T(8,128)(2,1)S(1)}, bf16[32,1024]{1,0:T(8,128)(2,1)S(1)}, u32[]{:S(2)}, u32[]{:S(2)}) collective-permute-start(bf16[32,1024]{1,0:T(8,128)(2,1)S(1)} %get-tuple-element.58), channel_id=1, source_target_pairs={{0,2},{2,0},{1,3},{3,1},{4,6},{6,4},{5,7},{7,5},{8,10},{10,8},{9,1... | collective-permute-start | bytes 196616 | tf_op jit(solution)/shard_map/ppermute | solution.py:709
where the time goes:
time: 79.7 us; the launch traced here: 79.6 us
  waiting for transfers between devices  30.5 us (38%)
  starting transfers between devices  26.4 us (33%)
  Pallas kernels  18.4 us (23%)
  other arithmetic  2.39 us (3%)
  local copies, waits for them, and re-layouts  1.61 us (2%)
    ppermute x12, waiting for transfers between devices, hop(): return lax.ppermute(x, 'roll', [(n, n ^ k) for n in range(roll)])  26.5 us
    ppermute x12, starting transfers between devices, hop(): return lax.ppermute(x, 'roll', [(n, n ^ k) for n in range(roll)])  22.5 us
    pallas_call x2, Pallas kernels, project(): pl.pallas_call(functools.partial(project_kernel, flip), out_shape=jax.Sha...  8.08 us
    pallas_call x1, Pallas kernels, prefix_attention(): pl.pallas_call(functools.partial(prefix_kernel, scale, roll), grid_spec=p...  4.22 us
    ppermute x1, waiting for transfers between devices, fast_body(): arrived = lax.ppermute(sent, 'tp', [(0, 1), (1, 0)])  2.78 us
    pallas_call x1, Pallas kernels, own_attention(): pl.pallas_call(functools.partial(own_kernel, scale, guess), grid_spec=plt...  2.64 us
    pallas_call x1, Pallas kernels, output(): pl.pallas_call(functools.partial(output_kernel, roll), in_specs=[vmem] *...  2.42 us
    ppermute x9, starting transfers between devices, across(): return lax.ppermute(x, 'seq', [(0, 1), (1, 0)])  2.35 us
  transfers between devices with their start and end apart: 22, of which 12 were waited for; matrix products, arithmetic and copies ran while one was open for 1% of the time, Pallas kernels for 9%

commit v1 on v0

--- a/solution.py
+++ b/solution.py
@@ -205,52 +205,69 @@
     return summed.astype(jnp.bfloat16)
 
 
-VMEM_MOST = 66900000
+SEND_LIMIT = 12 << 20
+LOG2E = 1.4426950408889634
 
 
 def contract_last(a, b):
     return lax.dot_general(a, b, (((1,), (1,)), ((), ())), preferred_element_type=jnp.float32)
 
 
-def project_kernel(flip, x_ref, wq_ref, wk_ref, wv_ref, out_ref, x_all, wq, wk, wv, sems):
+def place(out_ref, part, at, block):
     zone = lax.axis_index("roll")
-    seq = lax.axis_index("seq")
-    half = 1 - seq if flip else seq
-    roll, kh, block, width = out_ref.shape
+    roll, _, _, width = out_ref.shape
+    j, at = at // width, at % width
+    for b in range(roll):
+        out_ref[b ^ zone, j, :, at : at + part.shape[1]] = part[b * block : (b + 1) * block]
+
+
+def place_all(x, weights, out_ref, ready):
+    *wq, wk, wv = weights
+    _, kh, block, width = out_ref.shape
+    chunks = len(wq)
+    span = wq[0].shape[1]
     wide = width - 2 * HD
-    chunks = wq.shape[0]
-    span = wq.shape[2]
-
-    fetch = pltpu.make_async_copy(x_ref, x_all, sems.at[chunks + 2])
-    fetch.start()
-    copies = []
     for c in range(chunks):
-        at = pl.multiple_of(half * (kh * wide) + c * span, span)
-        copies.append(pltpu.make_async_copy(wq_ref.at[:, pl.ds(at, span)], wq.at[c], sems.at[c]))
-    at = pl.multiple_of(half * (kh * HD), kh * HD)
-    copies.append(pltpu.make_async_copy(wk_ref.at[:, pl.ds(at, kh * HD)], wk, sems.at[chunks]))
-    copies.append(pltpu.make_async_copy(wv_ref.at[:, pl.ds(at, kh * HD)], wv, sems.at[chunks + 1]))
-    for copy in copies:
-        copy.start()
-    fetch.wait()
-    x = x_all[...]
-
-    def place(part, j, at):
-        for b in range(roll):
-            out_ref[b ^ zone, j, :, at : at + part.shape[1]] = part[b * block : (b + 1) * block]
-
-    for c in range(chunks):
-        copies[c].wait()
-        part = jnp.dot(x, wq[c], preferred_element_type=jnp.float32)
-        place(part, c * span // wide, c * span % wide)
-    for copy, w, at in ((copies[chunks], wk, wide), (copies[chunks + 1], wv, wide + HD)):
-        copy.wait()
+        ready(c)
+        part = jnp.dot(x, wq[c][...], preferred_element_type=jnp.float32)
+        place(out_ref, part, c * span // wide * width + c * span % wide, block)
+    for c, w, at in ((chunks, wk, wide), (chunks + 1, wv, wide + HD)):
+        ready(c)
         part = jnp.dot(x, w[...], preferred_element_type=jnp.float32)
         for j in range(kh):
-            place(part[:, j * HD : (j + 1) * HD], j, at)
-
-
-def project(hidden, w_query, w_key, w_value, roll, kh, flip):
+            place(out_ref, part[:, j * HD : (j + 1) * HD], j * width + at, block)
+
+
+def project_kernel(x_ref, wq_ref, wk_ref, wv_ref, send_ref, keep_ref, x_all, *refs):
+    seq = lax.axis_index("seq")
+    sems = refs[-1]
+    count = len(refs) // 2
+    sources = [wq_ref] * (count - 2) + [wk_ref, wv_ref]
+
+    def copies(half, targets, at):
+        made = []
+        for n, (source, target) in enumerate(zip(sources, targets)):
+            span = target.shape[1]
+            start = half * (source.shape[1] // 2) + (n * span if n < count - 2 else 0)
+            part = source.at[:, pl.ds(pl.multiple_of(start, span), span)]
+            made.append(pltpu.make_async_copy(part, target, sems.at[at + n]))
+        return made
+
+    fetch = pltpu.make_async_copy(x_ref, x_all, sems.at[2 * count])
+    fetch.start()
+    work = []
+    for half, out_ref, at in ((1 - seq, send_ref, 0), (seq, keep_ref, count)):
+        targets = refs[at : at + count]
+        started = copies(half, targets, at)
+        for copy in started:
+            copy.start()
+        work.append((targets, out_ref, started))
+    fetch.wait()
+    for targets, out_ref, started in work:
+        place_all(x_all[...], targets, out_ref, lambda c: started[c].wait())
+
+
+def project(hidden, w_query, w_key, w_value, roll, kh):
     rows, depth = hidden.shape
     kv_heads = w_key.shape[1] // HD
     wide = w_query.shape[1] // kv_heads
@@ -260,45 +277,47 @@
     chunks = kh * wide // span
     hbm = pl.BlockSpec(memory_space=pltpu.HBM)
     vmem = pl.BlockSpec(memory_space=pltpu.VMEM)
+    shapes = ([(depth, span)] * chunks + [(depth, kh * HD)] * 2) * 2
+    out = jax.ShapeDtypeStruct((roll, kh, block, width), jnp.float32)
     return pl.pallas_call(
-        functools.partial(project_kernel, flip),
-        out_shape=jax.ShapeDtypeStruct((roll, kh, block, width), jnp.float32),
+        project_kernel,
+        out_shape=[out, out],
         in_specs=[hbm] * 4,
-        out_specs=vmem,
-        scratch_shapes=[
-            pltpu.VMEM((rows, depth), jnp.bfloat16),
-            pltpu.VMEM((chunks, depth, span), jnp.bfloat16),
-            pltpu.VMEM((depth, kh * HD), jnp.bfloat16),
-            pltpu.VMEM((depth, kh * HD), jnp.bfloat16),
-            pltpu.SemaphoreType.DMA((chunks + 3,)),
-        ],
-        compiler_params=pltpu.CompilerParams(vmem_limit_bytes=VMEM_MOST - 4 * rows * width * kh),
+        out_specs=[vmem, vmem],
+        scratch_shapes=[pltpu.VMEM((rows, depth), jnp.bfloat16)]
+        + [pltpu.VMEM(s, jnp.bfloat16) for s in shapes]
+        + [pltpu.SemaphoreType.DMA((len(shapes) + 1,))],
+        compiler_params=pltpu.CompilerParams(vmem_limit_bytes=SEND_LIMIT),
         cost_estimate=pl.CostEstimate(
-            flops=2 * rows * depth * width * kh,
-            bytes_accessed=2 * depth * width * kh + 4 * rows * width * kh,
-            transcendentals=0,
-        ),
-        name="project_send" if flip else "project_keep",
-    )(hidden, w_query, w_key, w_value)
-
-
-def finish_kernel(group, per, meta, keep_ref, got_ref, *refs):
-    others = refs[:-8]
+            flops=4 * rows * depth * width * kh, bytes_accessed=4 * depth * width * kh, transcendentals=0
+        ),
+        name="project",
+    )(*[pltpu.with_memory_space_constraint(a, pltpu.HBM) for a in (hidden, w_query, w_key, w_value)])
+
+
+def finish_kernel(group, per, kh, *refs):
     bq_ref, bk_ref, bv_ref, cos_ref, sin_ref, q_ref, k_ref, v_ref = refs[-8:]
-    kh = keep_ref.shape[1]
-    guess = cos_ref.shape[0] // per
-    cosine = cos_ref[...]
-    sine = sin_ref[...]
+    sums = refs[:-8]
+    block = sums[0].shape[1]
+    guess = block // per
+    seq = lax.axis_index("seq")
+    rows = pl.ds(pl.multiple_of(lax.axis_index("roll") * block, block), block)
+    cosine = cos_ref[rows, :]
+    sine = sin_ref[rows, :]
+
+    def bias_of(ref, n):
+        at = seq * (ref.shape[1] // 2) + n * HD
+        return ref[:, pl.ds(pl.multiple_of(at, HD), HD)]
 
     def total(j, g):
         at = slice(g * HD, (g + 1) * HD)
-        u = keep_ref[0, j, :, at] + got_ref[0, j, :, at]
-        for o in others:
+        u = sums[0][j, :, at]
+        for o in sums[1:]:
             u = u + o[j, :, at]
         if g < group:
-            bias = bq_ref[:, (j * group + g) * HD : (j * group + g + 1) * HD]
+            bias = bias_of(bq_ref, j * group + g)
         else:
-            bias = (bk_ref if g == group else bv_ref)[:, j * HD : (j + 1) * HD]
+            bias = bias_of(bk_ref if g == group else bv_ref, j)
         return u + bias.astype(jnp.float32)
 
     def turn(u):
@@ -316,29 +335,15 @@
         v_ref[j] = total(j, group + 1).astype(jnp.bfloat16)
 
 
-def finish(meta, keep, got, others, biases, cosine, sine, per):
-    _, kh, block, width = keep.shape
+def finish(sums, biases, cosine, sine, per):
+    kh, block, width = sums[0].shape
     group = width // HD - 2
     guess = block // per
-    first = pl.BlockSpec((1, kh, block, width), lambda n, meta: (0, 0, 0, 0))
-    part = pl.BlockSpec((kh, block, width), lambda n, meta: (0, 0, 0))
-    table = pl.BlockSpec((block, HD), lambda n, meta: (meta[0], 0))
-
-    def half(bias):
-        return pl.BlockSpec((1, bias.shape[1] // 2), lambda n, meta: (0, meta[1]))
-
+    vmem = pl.BlockSpec(memory_space=pltpu.VMEM)
     return pl.pallas_call(
-        functools.partial(finish_kernel, group, per),
-        grid_spec=pltpu.PrefetchScalarGridSpec(
-            num_scalar_prefetch=1,
-            grid=(1,),
-            in_specs=[first, first] + [part] * len(others) + [half(b) for b in biases] + [table, table],
-            out_specs=(
-                pl.BlockSpec((per, kh, group * guess, HD), lambda n, meta: (0, 0, 0, 0)),
-                pl.BlockSpec((kh, block, HD), lambda n, meta: (0, 0, 0)),
-                pl.BlockSpec((kh, block, HD), lambda n, meta: (0, 0, 0)),
-            ),
-        ),
+        functools.partial(finish_kernel, group, per, kh),
+        in_specs=[vmem] * (len(sums) + len(biases) + 2),
+        out_specs=[vmem] * 3,
         out_shape=(
             jax.ShapeDtypeStruct((per, kh, group * guess, HD), jnp.bfloat16),
             jax.ShapeDtypeStruct((kh, block, HD), jnp.bfloat16),
@@ -346,67 +351,61 @@
         ),
         compiler_params=pltpu.CompilerParams(vmem_limit_bytes=16 << 20),
         name="finish",
-    )(meta, keep, got, *others, *biases, cosine, sine)
-
-
-def own_kernel(scale, guess, meta, lengths, q_ref, kn_ref, vn_ref, k0_ref, k1_ref, v0_ref, v1_ref, n_ref, m_ref, l_ref):
+    )(*sums, *biases, cosine, sine)
+
+
+def own_kernel(scale, guess, lengths, q_ref, kn_ref, vn_ref, k0_ref, k1_ref, v0_ref, v1_ref, n_ref, m_ref, l_ref):
     per, kh, width, _ = q_ref.shape
     span = k0_ref.shape[1]
-    seq = meta[1]
+    seq = lax.axis_index("seq")
+    zone = lax.axis_index("roll")
     fresh = kn_ref.shape[1]
     key_id = lax.broadcasted_iota(jnp.int32, (width, span), 1)
     new_id = lax.broadcasted_iota(jnp.int32, (width, fresh), 1)
     row_id = lax.broadcasted_iota(jnp.int32, (width, fresh), 0) % guess
     for i in range(per):
-        length = lengths[meta[0] * per + i]
+        length = lengths[zone * per + i]
         sees = (key_id < length - seq * span, key_id < length - (1 - seq) * span)
         causal = (new_id >= i * guess) & (new_id - i * guess <= row_id)
         sees = sees + (causal,)
         for j in range(kh):
             q = q_ref[i, j]
-            at = slice(j * HD, (j + 1) * HD)
+            at = pl.ds(pl.multiple_of((seq * kh + j) * HD, HD), HD)
             keys = (k0_ref[i, :, at], k1_ref[i, :, at], kn_ref[j])
             values = (v0_ref[i, :, at], v1_ref[i, :, at], vn_ref[j])
-            scores = [jnp.where(see, contract_last(q, k) * scale, NEG_FILL) for k, see in zip(keys, sees)]
+            scores = [jnp.where(see, contract_last(q, k), NEG_FILL) for k, see in zip(keys, sees)]
             peak = jnp.max(scores[0], axis=1, keepdims=True)
             for s in scores[1:]:
                 peak = jnp.maximum(peak, jnp.max(s, axis=1, keepdims=True))
             total = jnp.zeros((width, 1), jnp.float32)
             numer = jnp.zeros((width, HD), jnp.float32)
             for s, v in zip(scores, values):
-                w = jnp.exp(s - peak)
+                w = jnp.exp2((s - peak) * (scale * LOG2E))
                 total = total + jnp.sum(w, axis=1, keepdims=True)
                 numer = numer + jnp.dot(w.astype(jnp.bfloat16), v, preferred_element_type=jnp.float32)
+            peak = peak * scale
             n_ref[i, j] = numer
             m_ref[i, j] = jnp.broadcast_to(peak, (width, HD))
             l_ref[i, j] = jnp.broadcast_to(total, (width, HD))
 
 
-def own_attention(meta, lengths, q, k_new, v_new, keys, keys_got, values, values_got, scale, guess):
+def own_attention(lengths, q, k_new, v_new, keys, keys_got, values, values_got, scale, guess):
     per, kh, width, _ = q.shape
     span = keys.shape[1]
-    cols = kh * HD
-    local = pl.BlockSpec((per, span, cols), lambda n, meta, lengths: (0, 0, meta[1]))
-    got = pl.BlockSpec((per, span, cols), lambda n, meta, lengths: (0, 0, 0))
-    fresh = pl.BlockSpec(k_new.shape, lambda n, meta, lengths: (0, 0, 0))
-    whole = pl.BlockSpec(q.shape, lambda n, meta, lengths: (0, 0, 0, 0))
+    vmem = pl.BlockSpec(memory_space=pltpu.VMEM)
     out = jax.ShapeDtypeStruct(q.shape, jnp.float32)
     elements = per * kh * width * span * 2
     return pl.pallas_call(
         functools.partial(own_kernel, scale, guess),
-        grid_spec=pltpu.PrefetchScalarGridSpec(
-            num_scalar_prefetch=2,
-            grid=(1,),
-            in_specs=[whole, fresh, fresh, local, got, local, got],
-            out_specs=(whole, whole, whole),
-        ),
+        in_specs=[pl.BlockSpec(memory_space=pltpu.SMEM)] + [vmem] * 7,
+        out_specs=[vmem] * 3,
         out_shape=(out, out, out),
-        compiler_params=pltpu.CompilerParams(vmem_limit_bytes=24 << 20),
+        compiler_params=pltpu.CompilerParams(vmem_limit_bytes=12 << 20),
         cost_estimate=pl.CostEstimate(
-            flops=4 * elements * HD, bytes_accessed=8 * per * span * cols, transcendentals=elements
+            flops=4 * elements * HD, bytes_accessed=8 * per * span * kh * HD, transcendentals=elements
         ),
         name="own_attention",
-    )(meta, lengths, q, k_new, v_new, keys, keys_got, values, values_got)
+    )(lengths, q, k_new, v_new, keys, keys_got, values, values_got)
 
 
 def split_three(x):
@@ -416,108 +415,103 @@
     return high, middle, rest - middle
 
 
-def prefix_kernel(scale, roll, meta, prompts, *refs):
+def prefix_kernel(scale, roll, prompts, *refs):
     q_refs = refs[:roll]
     k0_ref, k1_ref, v0_ref, v1_ref, on_ref, om_ref, ol_ref = refs[roll : roll + 7]
     n_out, m_out, l_out = refs[roll + 7 : roll + 10]
     packed = refs[roll + 10 : 2 * roll + 9]
     q_all, n_all, m_all, l_all, order = refs[2 * roll + 9 :]
     per, kh, width, _ = q_refs[0].shape
-    prompt = pl.program_id(0)
-    j = pl.program_id(1)
-    share = roll * per // pl.num_programs(0)
-
-    @pl.when((prompt == 0) & (j == 0))
-    def _():
-        for k in range(roll):
-            q_all[k * per : (k + 1) * per] = q_refs[k][...]
-
-    @pl.when(j == 0)
-    def _():
-        filled = jnp.int32(0)
-        for k in range(roll):
-            for i in range(per):
-                chosen = prompts[(meta[0] ^ k) * per + i] == prompt
+    zone = lax.axis_index("roll")
+    seq = lax.axis_index("seq")
+    count = k0_ref.shape[0]
+    share = roll * per // count
+
+    for k in range(roll):
+        q_all[k * per : (k + 1) * per] = q_refs[k][...]
+    filled = [jnp.int32(p * share) for p in range(count)]
+    for k in range(roll):
+        for i in range(per):
+            owner = prompts[(zone ^ k) * per + i]
+            for p in range(count):
+                chosen = owner == p
 
                 @pl.when(chosen)
                 def _():
-                    order[filled] = k * per + i
-
-                filled = filled + chosen.astype(jnp.int32)
-
-    ids = [order[n] for n in range(share)]
-    q = jnp.concatenate([q_all[at, j] for at in ids], axis=0)
-    scores = [contract_last(q, k_ref[0]) * scale for k_ref in (k0_ref, k1_ref)]
-    peak = jnp.maximum(
-        jnp.max(scores[0], axis=1, keepdims=True), jnp.max(scores[1], axis=1, keepdims=True)
-    )
-    total = jnp.zeros(peak.shape, jnp.float32)
-    numer = jnp.zeros((share * width, HD), jnp.float32)
-    for s, v_ref in zip(scores, (v0_ref, v1_ref)):
-        w = jnp.exp(s - peak)
-        total = total + jnp.sum(w, axis=1, keepdims=True)
-        numer = numer + jnp.dot(w.astype(jnp.bfloat16), v_ref[0], preferred_element_type=jnp.float32)
-    peak = jnp.broadcast_to(peak, numer.shape)
-    total = jnp.broadcast_to(total, numer.shape)
-    for n, at in enumerate(ids):
-        span = slice(n * width, (n + 1) * width)
-        n_all[at, j] = numer[span]
-        m_all[at, j] = peak[span]
-        l_all[at, j] = total[span]
-
-    @pl.when((prompt == pl.num_programs(0) - 1) & (j == kh - 1))
-    def _():
+                    order[filled[p]] = k * per + i
+
+                filled[p] = filled[p] + chosen.astype(jnp.int32)
+
+    for p in range(count):
+        ids = [order[p * share + n] for n in range(share)]
+        for j in range(kh):
+            at = pl.ds(pl.multiple_of((seq * kh + j) * HD, HD), HD)
+            q = jnp.concatenate([q_all[n, j] for n in ids], axis=0)
+            scores = [contract_last(q, k_ref[p, :, at]) for k_ref in (k0_ref, k1_ref)]
+            peak = jnp.maximum(
+                jnp.max(scores[0], axis=1, keepdims=True), jnp.max(scores[1], axis=1, keepdims=True)
+            )
+            total = jnp.zeros(peak.shape, jnp.float32)
+            numer = jnp.zeros((share * width, HD), jnp.float32)
+            for s, v_ref in zip(scores, (v0_ref, v1_ref)):
+                w = jnp.exp2((s - peak) * (scale * LOG2E))
+                total = total + jnp.sum(w, axis=1, keepdims=True)
+                numer = numer + jnp.dot(
+                    w.astype(jnp.bfloat16), v_ref[p, :, at], preferred_element_type=jnp.float32
+                )
+            peak = jnp.broadcast_to(peak * scale, numer.shape)
+            total = jnp.broadcast_to(total, numer.shape)
+            for n, to in enumerate(ids):
+                span = slice(n * width, (n + 1) * width)
+                n_all[to, j] = numer[span]
+                m_all[to, j] = peak[span]
+                l_all[to, j] = total[span]
+
+    for i in range(per):
+        for h in range(kh):
+            m_a, m_b = m_all[i, h], om_ref[i, h]
+            peak = jnp.maximum(m_a, m_b)
+            f_a, f_b = jnp.exp(m_a - peak), jnp.exp(m_b - peak)
+            m_out[i, h] = peak
+            l_out[i, h] = l_all[i, h] * f_a + ol_ref[i, h] * f_b
+            n_out[i, h] = n_all[i, h] * f_a + on_ref[i, h] * f_b
+    lane = lax.broadcasted_iota(jnp.int32, (width, HD), 1)
+    for k in range(1, roll):
+        stats = jnp.zeros((width, HD), jnp.float32)
         for i in range(per):
             for h in range(kh):
-                m_a, m_b = m_all[i, h], om_ref[i, h]
-                peak = jnp.maximum(m_a, m_b)
-                f_a, f_b = jnp.exp(m_a - peak), jnp.exp(m_b - peak)
-                m_out[i, h] = peak
-                l_out[i, h] = l_all[i, h] * f_a + ol_ref[i, h] * f_b
-                n_out[i, h] = n_all[i, h] * f_a + on_ref[i, h] * f_b
-        lane = lax.broadcasted_iota(jnp.int32, (width, HD), 1)
-        for k in range(1, roll):
-            stats = jnp.zeros((width, HD), jnp.float32)
-            for i in range(per):
-                for h in range(kh):
-                    u = i * kh + h
-                    packed[k - 1][u * width : (u + 1) * width, :] = n_all[k * per + i, h].astype(jnp.bfloat16)
-                    pieces = split_three(m_all[k * per + i, h]) + split_three(l_all[k * per + i, h])
-                    for c, piece in enumerate(pieces):
-                        stats = jnp.where(lane == 6 * u + c, piece, stats)
-            u = per * kh
-            packed[k - 1][u * width : (u + 1) * width, :] = stats.astype(jnp.bfloat16)
-
-
-def prefix_attention(meta, prompt_of, queries, keys, keys_got, values, values_got, own, scale):
+                u = i * kh + h
+                packed[k - 1][u * width : (u + 1) * width, :] = n_all[k * per + i, h].astype(jnp.bfloat16)
+                pieces = split_three(m_all[k * per + i, h]) + split_three(l_all[k * per + i, h])
+                for c, piece in enumerate(pieces):
+                    stats = jnp.where(lane == 6 * u + c, piece, stats)
+        u = per * kh
+        packed[k - 1][u * width : (u + 1) * width, :] = stats.astype(jnp.bfloat16)
+
+
+def prefix_attention(prompt_of, queries, keys, keys_got, values, values_got, own, scale):
     roll = len(queries)
     per, kh, width, _ = queries[0].shape
     prompts, span, _ = keys.shape
-    local = pl.BlockSpec((1, span, HD), lambda p, j, meta, prompts: (p, 0, meta[1] * kh + j))
-    got = pl.BlockSpec((1, span, HD), lambda p, j, meta, prompts: (p, 0, j))
-    whole = pl.BlockSpec(queries[0].shape, lambda p, j, meta, prompts: (0, 0, 0, 0))
+    vmem = pl.BlockSpec(memory_space=pltpu.VMEM)
     rows = (per * kh + 1) * width
-    sent = pl.BlockSpec((rows, HD), lambda p, j, meta, prompts: (0, 0))
     out = jax.ShapeDtypeStruct(queries[0].shape, jnp.float32)
     elements = roll * per * kh * width * span * 2
     everything = (roll * per, kh, width, HD)
     outs = pl.pallas_call(
         functools.partial(prefix_kernel, scale, roll),
-        grid_spec=pltpu.PrefetchScalarGridSpec(
-            num_scalar_prefetch=2,
-            grid=(prompts, kh),
-            in_specs=[whole] * roll + [local, got, local, got] + [whole] * 3,
-            out_specs=[whole] * 3 + [sent] * (roll - 1),
-            scratch_shapes=[pltpu.VMEM(everything, jnp.bfloat16)] + [pltpu.VMEM(everything, jnp.float32)] * 3
-            + [pltpu.SMEM((roll * per,), jnp.int32)],
-        ),
+        in_specs=[pl.BlockSpec(memory_space=pltpu.SMEM)] + [vmem] * (roll + 7),
+        out_specs=[vmem] * (roll + 2),
+        scratch_shapes=[pltpu.VMEM(everything, jnp.bfloat16)]
+        + [pltpu.VMEM(everything, jnp.float32)] * 3
+        + [pltpu.SMEM((roll * per,), jnp.int32)],
         out_shape=[out] * 3 + [jax.ShapeDtypeStruct((rows, HD), jnp.bfloat16)] * (roll - 1),
-        compiler_params=pltpu.CompilerParams(vmem_limit_bytes=24 << 20),
+        compiler_params=pltpu.CompilerParams(vmem_limit_bytes=12 << 20),
         cost_estimate=pl.CostEstimate(
             flops=4 * elements * HD, bytes_accessed=8 * prompts * span * kh * HD, transcendentals=elements
         ),
         name="prefix_attention",
-    )(meta, prompt_of, *queries, keys, keys_got, values, values_got, *own)
+    )(prompt_of, *queries, keys, keys_got, values, values_got, *own)
     return outs[:3], outs[3:]
 
 
@@ -569,62 +563,53 @@
     )(*own, *packed)
 
 
-def output_kernel(roll, *refs):
-    parts = (refs[:roll], refs[roll : 2 * roll])
-    w_ref, keep_ref, send_ref, w, lhs, sems = refs[2 * roll :]
+def output_kernel(roll, theirs, *refs):
+    parts, w_ref, rest = refs[:roll], refs[roll], refs[roll + 1 :]
+    lhs = rest[-1]
     zone, seq, tp = lax.axis_index("roll"), lax.axis_index("seq"), lax.axis_index("tp")
-    block, cols = parts[0][0].shape
-    chunks, depth, _ = w.shape
-    each = chunks // 2
-    copies = []
-    for c in range(chunks):
-        side = seq if c < each else 1 - seq
-        at = pl.multiple_of(side * cols + (c % each) * depth, depth)
-        copies.append(pltpu.make_async_copy(w_ref.at[pl.ds(at, depth), :], w.at[c], sems.at[c]))
-    for copy in copies:
-        copy.start()
-    for h in range(2):
-        for k in range(roll):
-            at = pl.multiple_of((zone ^ k ^ (tp * (roll // 2))) * block, block)
-            lhs[h, pl.ds(at, block), :] = parts[h][k][...]
-    total = None
-    for c in range(chunks):
-        copies[c].wait()
-        at = (c % each) * depth
-        part = jnp.dot(lhs[c // each, :, at : at + depth], w[c], preferred_element_type=jnp.float32)
-        total = part if c == 0 else total + part
+    block, cols = parts[0].shape
+    side = 1 - seq if theirs else seq
+    for k in range(roll):
+        at = pl.multiple_of((zone ^ k ^ (tp * (roll // 2))) * block, block)
+        lhs[pl.ds(at, block), :] = parts[k][...]
+    w = w_ref[pl.ds(pl.multiple_of(side * cols, cols), cols), :]
+    part = jnp.dot(lhs[...], w, preferred_element_type=jnp.float32)
+    if not theirs:
+        rest[0][...] = part
+        return
+    part = rest[0][...] + part
+    keep_ref, send_ref = rest[1:3]
     rows = keep_ref.shape[0]
-    keep_ref[...] = total[:rows]
-    send_ref[...] = total[rows:].astype(send_ref.dtype)
-
-
-def output(mine, theirs, w_out):
-    roll = len(mine)
-    block, cols = mine[0].shape
-    depth = 512 if cols % 512 == 0 else cols
-    chunks = 2 * cols // depth
+    keep_ref[...] = part[:rows]
+    send_ref[...] = part[rows:].astype(send_ref.dtype)
+
+
+def output(parts, w_out, before=None):
+    roll = len(parts)
+    block, cols = parts[0].shape
     width = w_out.shape[1]
     rows = roll * block
     vmem = pl.BlockSpec(memory_space=pltpu.VMEM)
-    return pl.pallas_call(
-        functools.partial(output_kernel, roll),
-        in_specs=[vmem] * (2 * roll) + [pl.BlockSpec(memory_space=pltpu.HBM)],
-        out_specs=(vmem, vmem),
-        scratch_shapes=[
-            pltpu.VMEM((chunks, depth, width), jnp.bfloat16),
-            pltpu.VMEM((2, rows, cols), jnp.bfloat16),
-            pltpu.SemaphoreType.DMA((chunks,)),
-        ],
-        out_shape=(
+    theirs = before is not None
+    if theirs:
+        shapes = [
             jax.ShapeDtypeStruct((rows // 2, width), jnp.float32),
             jax.ShapeDtypeStruct((rows // 2, width), jnp.bfloat16),
-        ),
-        compiler_params=pltpu.CompilerParams(vmem_limit_bytes=24 << 20),
+        ]
+    else:
+        shapes = jax.ShapeDtypeStruct((rows, width), jnp.float32)
+    return pl.pallas_call(
+        functools.partial(output_kernel, roll, theirs),
+        in_specs=[vmem] * (roll + 1 + theirs),
+        out_specs=[vmem, vmem] if theirs else vmem,
+        scratch_shapes=[pltpu.VMEM((rows, cols), jnp.bfloat16)],
+        out_shape=shapes,
+        compiler_params=pltpu.CompilerParams(vmem_limit_bytes=16 << 20),
         cost_estimate=pl.CostEstimate(
-            flops=4 * rows * cols * width, bytes_accessed=4 * cols * width, transcendentals=0
-        ),
-        name="output",
-    )(*mine, *theirs, w_out)
+            flops=2 * rows * cols * width, bytes_accessed=2 * cols * width, transcendentals=0
+        ),
+        name="output_theirs" if theirs else "output_mine",
+    )(*parts, w_out, *((before,) if theirs else ()))
 
 
 def fast_body(
@@ -651,9 +636,6 @@
     block = hidden.shape[0] // roll
     guess = block // per
     scale = 1.0 / math.sqrt(HD)
-    zone = lax.axis_index("roll").astype(jnp.int32)
-    seq = lax.axis_index("seq").astype(jnp.int32)
-    tp = lax.axis_index("tp").astype(jnp.int32)
 
     def across(x):
         return lax.ppermute(x, "seq", [(0, 1), (1, 0)])
@@ -665,20 +647,17 @@
         sent = {k: hop(pick(k), k) for k in reversed(range(1, roll))}
         return [sent[k] for k in range(1, roll)]
 
-    send = project(hidden, w_query, w_key, w_value, roll, kh, True)
+    send, keep = project(hidden, w_query, w_key, w_value, roll, kh)
     got = across(send)
-    keep = project(hidden, w_query, w_key, w_value, roll, kh, False)
-    terms = tuple(keep[k] + got[k] for k in range(1, roll))
+    terms = [keep[k] + got[k] for k in range(roll)]
+    sums = [terms[0]] + hops(lambda k: terms[k])
     caches = (suffix_keys, suffix_values, prefix_keys, prefix_values)
-    terms, small = lax.optimization_barrier((terms, (suffix_lengths, b_query, b_key, b_value, zone, seq, *caches)))
-    meta = jnp.stack(small[4:6])
-    sums = hops(lambda k: terms[k - 1])
-    caches = small[6:]
-
-    def other_half(x):
-        return across(lax.dynamic_slice_in_dim(x, (1 - seq) * (kh * HD), kh * HD, x.ndim - 1))
-
-    sk_got, sv_got, pk_got, pv_got = [other_half(x) for x in caches]
+    _, small = lax.optimization_barrier(
+        (terms[0], (suffix_lengths, b_query, b_key, b_value, *caches))
+    )
+    caches = small[4:]
+
+    sk_got, sv_got, pk_got, pv_got = [across(x) for x in caches]
 
     row_ids = jnp.arange(hidden.shape[0], dtype=jnp.int32)
     prefix_total = prefix_keys.shape[1] * roll * 2
@@ -693,19 +672,19 @@
     sine = jnp.concatenate([-sine, sine], axis=-1)
     biases = [b[None, :] for b in small[1:4]]
 
-    q, k_new, v_new = finish(meta, keep, got, sums, biases, cosine, sine, per)
+    q, k_new, v_new = finish(sums, biases, cosine, sine, per)
     queries = [q] + hops(lambda k: q)
     own = own_attention(
-        meta, suffix_lengths, q, k_new, v_new, suffix_keys, sk_got, suffix_values, sv_got, scale, guess
+        suffix_lengths, q, k_new, v_new, suffix_keys, sk_got, suffix_values, sv_got, scale, guess
     )
     own, packed = prefix_attention(
-        meta, prompt_of, queries, prefix_keys, pk_got, prefix_values, pv_got, own, scale
+        prompt_of, queries, prefix_keys, pk_got, prefix_values, pv_got, own, scale
     )
     packed = hops(lambda k: packed[k - 1])
     share = merge(own, packed, group)
     mine = [share] + hops(lambda k: share)
     theirs = [across(m) for m in mine]
-    kept, sent = output(mine, theirs, w_out)
+    kept, sent = output(theirs, w_out, output(mine, w_out))
     arrived = lax.ppermute(sent, "tp", [(0, 1), (1, 0)])
     return (kept + arrived.astype(jnp.float32)).astype(jnp.bfloat16)
 

time: 79.7 us -> 72.5 us (0.910)
  Pallas kernels: 18.4 us -> 12.8 us
  local copies, waits for them, and re-layouts: 1.61 us -> 0.07 us
  other arithmetic: 2.39 us -> 1.12 us
  waiting for transfers between devices: 30.5 us -> 31.6 us
    pallas_call x6, Pallas kernels: 18 us -> 12.4 us  [the longest x1 5.13 us: project(): pl.pallas_call(project_kernel, out_shape=[out, out], in_specs=[hbm] * 4,...]
    dynamic_slice x4 -> x0, local copies, waits for them, and re-layouts: 1.53 us -> none  [other_half(): lax.dynamic_slice_in_dim(x, (1 - seq) * (kh * HD), kh * HD, x.ndim - 1)]
    add x1, other arithmetic: 1.29 us -> 0.1 us  [fast_body(): terms = [keep[k] + got[k] for k in range(roll)]]
    ppermute x9, waiting for transfers between devices: 1.26 us -> 2.09 us  [across(): return lax.ppermute(x, 'seq', [(0, 1), (1, 0)])]
  transfers between devices with their start and end apart: 22 -> 22, of which waited for: 12 -> 12; matrix products, arithmetic and copies ran while one was open for 1% -> 1% of each run, Pallas kernels for 9% -> 5%
where the time goes in v1:
time: 72.5 us; the launch traced here: 72.3 us
  waiting for transfers between devices  31.6 us (44%)
  starting transfers between devices  26.5 us (37%)
  Pallas kernels  12.8 us (18%)
  other arithmetic  1.12 us (2%)
    ppermute x12, waiting for transfers between devices, hop(): return lax.ppermute(x, 'roll', [(n, n ^ k) for n in range(roll)])  26.7 us
    ppermute x12, starting transfers between devices, hop(): return lax.ppermute(x, 'roll', [(n, n ^ k) for n in range(roll)])  22.8 us
    pallas_call x1, Pallas kernels, project(): pl.pallas_call(project_kernel, out_shape=[out, out], in_specs=[hbm] * 4,...  5.13 us
    pallas_call x1, Pallas kernels, prefix_attention(): pl.pallas_call(functools.partial(prefix_kernel, scale, roll), in_specs=[p...  2.86 us
    ppermute x1, waiting for transfers between devices, fast_body(): arrived = lax.ppermute(sent, 'tp', [(0, 1), (1, 0)])  2.77 us
    pallas_call x1, Pallas kernels, own_attention(): pl.pallas_call(functools.partial(own_kernel, scale, guess), in_specs=[pl....  2.62 us
    ppermute x9, starting transfers between devices, across(): return lax.ppermute(x, 'seq', [(0, 1), (1, 0)])  2.17 us
    ppermute x9, waiting for transfers between devices, across(): return lax.ppermute(x, 'seq', [(0, 1), (1, 0)])  2.09 us
  transfers between devices with their start and end apart: 22, of which 12 were waited for; matrix products, arithmetic and copies ran while one was open for 1% of the time, Pallas kernels for 5%

profile of v1, /device:TPU:0, one launch (start us, length us, event | category | flops | bytes accessed | tf_op | source)
XLA Modules:
  0.0 72.3 jit_solution(6102616992149475847)
XLA Ops:
  0.0 5.1 %project.1 = (f32[4,2,16,1280]{3,2,1,0:T(8,128)S(1)}, f32[4,2,16,1280]{3,2,1,0:T(8,128)S(1)}) custom-call(bf16[64,1024]{1,0:T(8,128)(2,1)} %x_ref.1, bf16[1024,4096]{1,0:T(8,128)(2,1)} %wq_ref.1, bf16[1024,512]{1,0:T(8,128)(2,1)} %wk_ref.1, bf16[1024,512]{1,0:T(8,128)(2,1)} %wv_ref.1), custom_call_target="tpu_custom_call" | custom-call | flops 671088640 | bytes 10485760 | tf_op jit(solution)/shard_map/project/pallas_call | solution.py:282
  5.2 0.0 copy-start.7
  5.2 0.0 copy-start.8
  5.2 0.6 collective-permute-start
  5.8 1.7 %collective-permute-done = f32[4,2,16,1280]{3,2,1,0:T(8,128)S(1)} collective-permute-done((f32[4,2,16,1280]{3,2,1,0:T(8,128)S(1)}, f32[4,2,16,1280]{3,2,1,0:T(8,128)S(1)}, u32[]{:S(2)}, u32[]{:S(2)}) %collective-permute-start) | collective-permute-done | bytes 655392 | tf_op jit(solution)/shard_map/ppermute | solution.py:641
  7.5 0.1 fusion
  7.6 0.4 collective-permute-start.10
  8.0 0.1 collective-permute-start.9
  8.2 0.4 collective-permute-start.7
  8.5 0.1 collective-permute-start.8
  8.7 2.9 %collective-permute-start.1 = (f32[2,16,1280]{2,1,0:T(8,128)S(1)}, f32[2,16,1280]{2,1,0:T(8,128)S(1)}, u32[]{:S(2)}, u32[]{:S(2)}) collective-permute-start(f32[2,16,1280]{2,1,0:T(8,128)S(1)} %get-tuple-element.55), channel_id=1, source_target_pairs={{0,4},{4,0},{8,12},{12,8},{1,5},{5,1},{9,13},{13,9},{2,6},{6,2},{1... | collective-permute-start | bytes 491528 | tf_op jit(solution)/shard_map/ppermute | solution.py:644
  11.6 0.1 select_reduce_fusion
  11.7 4.4 %collective-permute-done.1.refs_1_ = f32[2,16,1280]{2,1,0:T(8,128)S(1)} collective-permute-done((f32[2,16,1280]{2,1,0:T(8,128)S(1)}, f32[2,16,1280]{2,1,0:T(8,128)S(1)}, u32[]{:S(2)}, u32[]{:S(2)}) %collective-permute-start.1) | collective-permute-done | bytes 163872 | tf_op jit(solution)/shard_map/ppermute | solution.py:644
  16.1 2.8 %collective-permute-start.2 = (f32[2,16,1280]{2,1,0:T(8,128)S(1)}, f32[2,16,1280]{2,1,0:T(8,128)S(1)}, u32[]{:S(2)}, u32[]{:S(2)}) collective-permute-start(f32[2,16,1280]{2,1,0:T(8,128)S(1)} %get-tuple-element.54), channel_id=1, source_target_pairs={{0,8},{4,12},{8,0},{12,4},{1,9},{5,13},{9,1},{13,5},{2,10},{6,14},... | collective-permute-start | bytes 491528 | tf_op jit(solution)/shard_map/ppermute | solution.py:644
  18.9 7.3 %collective-permute-done.2.refs_2_ = f32[2,16,1280]{2,1,0:T(8,128)S(1)} collective-permute-done((f32[2,16,1280]{2,1,0:T(8,128)S(1)}, f32[2,16,1280]{2,1,0:T(8,128)S(1)}, u32[]{:S(2)}, u32[]{:S(2)}) %collective-permute-start.2) | collective-permute-done | bytes 163872 | tf_op jit(solution)/shard_map/ppermute | solution.py:644
  26.2 3.4 %collective-permute-start.3 = (f32[2,16,1280]{2,1,0:T(8,128)S(1)}, f32[2,16,1280]{2,1,0:T(8,128)S(1)}, u32[]{:S(2)}, u32[]{:S(2)}) collective-permute-start(f32[2,16,1280]{2,1,0:T(8,128)S(1)} %get-tuple-element.53), channel_id=1, source_target_pairs={{0,12},{4,8},{8,4},{12,0},{1,13},{5,9},{9,5},{13,1},{2,14},{6,10},... | collective-permute-start | bytes 491528 | tf_op jit(solution)/shard_map/ppermute | solution.py:644
  29.6 0.2 fusion.4
  29.8 0.1 pad_maximum_fusion
  29.9 4.1 %collective-permute-done.3.refs_3_ = f32[2,16,1280]{2,1,0:T(8,128)S(1)} collective-permute-done((f32[2,16,1280]{2,1,0:T(8,128)S(1)}, f32[2,16,1280]{2,1,0:T(8,128)S(1)}, u32[]{:S(2)}, u32[]{:S(2)}) %collective-permute-start.3) | collective-permute-done | bytes 163872 | tf_op jit(solution)/shard_map/ppermute | solution.py:644
  34.1 0.1 finish.1
  34.2 2.4 %collective-permute-start.4 = (bf16[2,2,64,128]{3,2,1,0:T(8,128)(2,1)S(1)}, bf16[2,2,64,128]{3,2,1,0:T(8,128)(2,1)S(1)}, u32[]{:S(2)}, u32[]{:S(2)}) collective-permute-start(bf16[2,2,64,128]{3,2,1,0:T(8,128)(2,1)S(1)} %get-tuple-element.35.q_ref.refs_0_), channel_id=1, source_target_pairs={{0,4},{4,0},{8,12},{12,8},{1,5},{5,1},{9,13},{13,9},{2,6},{6,2},{1... | collective-permute-start | bytes 196616 | tf_op jit(solution)/shard_map/ppermute | solution.py:644
  36.6 1.7 %collective-permute-start.5 = (bf16[2,2,64,128]{3,2,1,0:T(8,128)(2,1)S(1)}, bf16[2,2,64,128]{3,2,1,0:T(8,128)(2,1)S(1)}, u32[]{:S(2)}, u32[]{:S(2)}) collective-permute-start(bf16[2,2,64,128]{3,2,1,0:T(8,128)(2,1)S(1)} %get-tuple-element.35.q_ref.refs_0_), channel_id=1, source_target_pairs={{0,8},{4,12},{8,0},{12,4},{1,9},{5,13},{9,1},{13,5},{2,10},{6,14},... | collective-permute-start | bytes 196616 | tf_op jit(solution)/shard_map/ppermute | solution.py:644
  38.3 0.8 %collective-permute-start.6 = (bf16[2,2,64,128]{3,2,1,0:T(8,128)(2,1)S(1)}, bf16[2,2,64,128]{3,2,1,0:T(8,128)(2,1)S(1)}, u32[]{:S(2)}, u32[]{:S(2)}) collective-permute-start(bf16[2,2,64,128]{3,2,1,0:T(8,128)(2,1)S(1)} %get-tuple-element.35.q_ref.refs_0_), channel_id=1, source_target_pairs={{0,12},{4,8},{8,4},{12,0},{1,13},{5,9},{9,5},{13,1},{2,14},{6,10},... | collective-permute-start | bytes 196616 | tf_op jit(solution)/shard_map/ppermute | solution.py:644
  39.0 2.6 %own_attention.1 = (f32[2,2,64,128]{3,2,1,0:T(8,128)S(1)}, f32[2,2,64,128]{3,2,1,0:T(8,128)S(1)}, f32[2,2,64,128]{3,2,1,0:T(8,128)S(1)}) custom-call(s32[8]{0:T(128)S(1)} %copy-done.4, bf16[2,2,64,128]{3,2,1,0:T(8,128)(2,1)S(1)} %get-tuple-element.35.q_ref.refs_0_, bf16[2,16,128]{2,1,0:T(8,128)(2,1)S(1)} %get-tuple-element.38.kn_ref, ...), custom_call_target="tpu_custom_call" | custom-call | flops 268435456 | bytes 4194304 | tf_op jit(solution)/shard_map/own_attention/pallas_call | solution.py:398
  41.7 1.3 %collective-permute-done.5.refs_2_ = bf16[2,2,64,128]{3,2,1,0:T(8,128)(2,1)S(1)} collective-permute-done((bf16[2,2,64,128]{3,2,1,0:T(8,128)(2,1)S(1)}, bf16[2,2,64,128]{3,2,1,0:T(8,128)(2,1)S(1)}, u32[]{:S(2)}, u32[]{:S(2)}) %collective-permute-start.5) | collective-permute-done | bytes 65568 | tf_op jit(solution)/shard_map/ppermute | solution.py:644
  43.0 1.4 %collective-permute-done.6.refs_3_ = bf16[2,2,64,128]{3,2,1,0:T(8,128)(2,1)S(1)} collective-permute-done((bf16[2,2,64,128]{3,2,1,0:T(8,128)(2,1)S(1)}, bf16[2,2,64,128]{3,2,1,0:T(8,128)(2,1)S(1)}, u32[]{:S(2)}, u32[]{:S(2)}) %collective-permute-start.6) | collective-permute-done | bytes 65568 | tf_op jit(solution)/shard_map/ppermute | solution.py:644
  44.4 0.0 collective-permute-done.7.refs_5_
  44.4 0.0 collective-permute-done.8.refs_7_
  44.4 2.9 %prefix_attention.1 = (f32[2,2,64,128]{3,2,1,0:T(8,128)S(1)}, f32[2,2,64,128]{3,2,1,0:T(8,128)S(1)}, f32[2,2,64,128]{3,2,1,0:T(8,128)S(1)}, bf16[320,128]{1,0:T(...) custom-call(s32[8]{0:T(128)S(1)} %copy-done.5, ...), custom_call_target="tpu_custom_call" | custom-call | flops 536870912 | bytes 2097152 | tf_op jit(solution)/shard_map/prefix_attention/pallas_call | solution.py:501
  47.3 0.1 collective-permute-start.11
  47.3 1.9 %collective-permute-start.12 = (bf16[320,128]{1,0:T(8,128)(2,1)S(1)}, bf16[320,128]{1,0:T(8,128)(2,1)S(1)}, u32[]{:S(2)}, u32[]{:S(2)}) collective-permute-start(bf16[320,128]{1,0:T(8,128)(2,1)S(1)} %get-tuple-element.49), channel_id=1, source_target_pairs={{0,8},{4,12},{8,0},{12,4},{1,9},{5,13},{9,1},{13,5},{2,10},{6,14},... | collective-permute-start | bytes 245768 | tf_op jit(solution)/shard_map/ppermute | solution.py:644
  49.3 2.4 %collective-permute-start.13 = (bf16[320,128]{1,0:T(8,128)(2,1)S(1)}, bf16[320,128]{1,0:T(8,128)(2,1)S(1)}, u32[]{:S(2)}, u32[]{:S(2)}) collective-permute-start(bf16[320,128]{1,0:T(8,128)(2,1)S(1)} %get-tuple-element.50), channel_id=1, source_target_pairs={{0,12},{4,8},{8,4},{12,0},{1,13},{5,9},{9,5},{13,1},{2,14},{6,10},... | collective-permute-start | bytes 245768 | tf_op jit(solution)/shard_map/ppermute | solution.py:644
  51.7 0.2 collective-permute-done.11.refs_0_
  51.9 3.8 %collective-permute-done.12.refs_1_ = bf16[320,128]{1,0:T(8,128)(2,1)S(1)} collective-permute-done((bf16[320,128]{1,0:T(8,128)(2,1)S(1)}, bf16[320,128]{1,0:T(8,128)(2,1)S(1)}, u32[]{:S(2)}, u32[]{:S(2)}) %collective-permute-start.12) | collective-permute-done | bytes 81952 | tf_op jit(solution)/shard_map/ppermute | solution.py:644
  55.6 0.4 merge.1.refs_0_
  56.0 1.5 %collective-permute-start.15 = (bf16[16,2048]{1,0:T(8,128)(2,1)S(1)}, bf16[16,2048]{1,0:T(8,128)(2,1)S(1)}, u32[]{:S(2)}, u32[]{:S(2)}) collective-permute-start(bf16[16,2048]{1,0:T(8,128)(2,1)S(1)} %merge.1.refs_0_), channel_id=1, source_target_pairs={{0,4},{4,0},{8,12},{12,8},{1,5},{5,1},{9,13},{13,9},{2,6},{6,2},{1... | collective-permute-start | bytes 196616 | tf_op jit(solution)/shard_map/ppermute | solution.py:644
  57.5 1.6 %collective-permute-start.17 = (bf16[16,2048]{1,0:T(8,128)(2,1)S(1)}, bf16[16,2048]{1,0:T(8,128)(2,1)S(1)}, u32[]{:S(2)}, u32[]{:S(2)}) collective-permute-start(bf16[16,2048]{1,0:T(8,128)(2,1)S(1)} %merge.1.refs_0_), channel_id=1, source_target_pairs={{0,8},{4,12},{8,0},{12,4},{1,9},{5,13},{9,1},{13,5},{2,10},{6,14},... | collective-permute-start | bytes 196616 | tf_op jit(solution)/shard_map/ppermute | solution.py:644
  59.1 1.4 %collective-permute-start.19 = (bf16[16,2048]{1,0:T(8,128)(2,1)S(1)}, bf16[16,2048]{1,0:T(8,128)(2,1)S(1)}, u32[]{:S(2)}, u32[]{:S(2)}) collective-permute-start(bf16[16,2048]{1,0:T(8,128)(2,1)S(1)} %merge.1.refs_0_), channel_id=1, source_target_pairs={{0,12},{4,8},{8,4},{12,0},{1,13},{5,9},{9,5},{13,1},{2,14},{6,10},... | collective-permute-start | bytes 196616 | tf_op jit(solution)/shard_map/ppermute | solution.py:644
  60.5 0.0 collective-permute-start.14
  60.5 0.5 collective-permute-start.16
  61.0 3.1 %collective-permute-done.17.refs_2_ = bf16[16,2048]{1,0:T(8,128)(2,1)S(1)} collective-permute-done((bf16[16,2048]{1,0:T(8,128)(2,1)S(1)}, bf16[16,2048]{1,0:T(8,128)(2,1)S(1)}, u32[]{:S(2)}, u32[]{:S(2)}) %collective-permute-start.17) | collective-permute-done | bytes 65568 | tf_op jit(solution)/shard_map/ppermute | solution.py:644
  64.1 1.1 %collective-permute-done.19.refs_3_ = bf16[16,2048]{1,0:T(8,128)(2,1)S(1)} collective-permute-done((bf16[16,2048]{1,0:T(8,128)(2,1)S(1)}, bf16[16,2048]{1,0:T(8,128)(2,1)S(1)}, u32[]{:S(2)}, u32[]{:S(2)}) %collective-permute-start.19) | collective-permute-done | bytes 65568 | tf_op jit(solution)/shard_map/ppermute | solution.py:644
  65.3 0.8 %output_mine.1.refs_5_ = f32[64,1024]{1,0:T(8,128)S(1)} custom-call(bf16[16,2048]{1,0:T(8,128)(2,1)S(1)} %merge.1.refs_0_, bf16[16,2048]{1,0:T(8,128)(2,1)S(1)} %collective-permute-done.15.refs_1_, bf16[16,2048]{1,0:T(8,128)(2,1)S(1)} %collective-permute-done.17.refs_2_, bf16[16,2048]{1,0:T(8,128)(2,1)S(1)} %collective-permute-done.19.refs_3_, ...), custom_call_target="tpu_custom_call" | custom-call | flops 268435456 | bytes 4194304 | tf_op jit(solution)/shard_map/output_mine/pallas_call | solution.py:601
  66.2 0.3 collective-permute-done.20.refs_3_
  66.5 0.8 %output_theirs.1 = (f32[32,1024]{1,0:T(8,128)S(1)}, bf16[32,1024]{1,0:T(8,128)(2,1)S(1)}) custom-call(bf16[16,2048]{1,0:T(8,128)(2,1)S(1)} %collective-permute-done.14.refs_0_, bf16[16,2048]{1,0:T(8,128)(2,1)S(1)} %collective-permute-done.16.refs_1_, bf16[16,2048]{1,0:T(8,128)(2,1)S(1)} %collective-permute-done.18.refs_2_, ...), custom_call_target="tpu_custom_call" | custom-call | flops 268435456 | bytes 4194304 | tf_op jit(solution)/shard_map/output_theirs/pallas_call | solution.py:601
  67.4 1.6 %collective-permute-start.21 = (bf16[32,1024]{1,0:T(8,128)(2,1)S(1)}, bf16[32,1024]{1,0:T(8,128)(2,1)S(1)}, u32[]{:S(2)}, u32[]{:S(2)}) collective-permute-start(bf16[32,1024]{1,0:T(8,128)(2,1)S(1)} %get-tuple-element.52), channel_id=1, source_target_pairs={{0,2},{2,0},{1,3},{3,1},{4,6},{6,4},{5,7},{7,5},{8,10},{10,8},{9,1... | collective-permute-start | bytes 196616 | tf_op jit(solution)/shard_map/ppermute | solution.py:688
  68.9 2.8 %collective-permute-done.21 = bf16[32,1024]{1,0:T(8,128)(2,1)S(1)} collective-permute-done((bf16[32,1024]{1,0:T(8,128)(2,1)S(1)}, bf16[32,1024]{1,0:T(8,128)(2,1)S(1)}, u32[]{:S(2)}, u32[]{:S(2)}) %collective-permute-start.21) | collective-permute-done | bytes 65568 | tf_op jit(solution)/shard_map/ppermute | solution.py:688
  71.7 0.6 add_convert_fusion
  (37 shorter events, 0.1 us)
Async XLA Ops:
  0.0 29.8 %copy-start.6 = (bf16[4096]{0:T(1024)(128)(2,1)S(1)}, bf16[4096]{0:T(1024)(128)(2,1)}, u32[]{:S(2)}) copy-start(bf16[4096]{0:T(1024)(128)(2,1)} %param.18) | copy-start | bytes 24580
  0.0 8.2 %copy-start.2 = (bf16[2,512,512]{2,1,0:T(8,128)(2,1)S(1)}, bf16[2,512,512]{2,1,0:T(8,128)(2,1)}, u32[]{:S(2)}) copy-start(bf16[2,512,512]{2,1,0:T(8,128)(2,1)} %refs_4_.3) | copy-start | bytes 3145732
  0.0 8.5 %copy-start.3 = (bf16[2,512,512]{2,1,0:T(8,128)(2,1)S(1)}, bf16[2,512,512]{2,1,0:T(8,128)(2,1)}, u32[]{:S(2)}) copy-start(bf16[2,512,512]{2,1,0:T(8,128)(2,1)} %refs_6_.1) | copy-start | bytes 3145732
  0.0 8.0 %copy-start = (bf16[2,1024,512]{2,1,0:T(8,128)(2,1)S(1)}, bf16[2,1024,512]{2,1,0:T(8,128)(2,1)}, u32[]{:S(2)}) copy-start(bf16[2,1024,512]{2,1,0:T(8,128)(2,1)} %k0_ref.1) | copy-start | bytes 6291460
  0.0 7.6 %copy-start.1 = (bf16[2,1024,512]{2,1,0:T(8,128)(2,1)S(1)}, bf16[2,1024,512]{2,1,0:T(8,128)(2,1)}, u32[]{:S(2)}) copy-start(bf16[2,1024,512]{2,1,0:T(8,128)(2,1)} %v0_ref.1) | copy-start | bytes 6291460
  0.0 11.6 %copy-start.4 = (s32[8]{0:T(128)S(1)}, s32[8]{0:T(128)}, u32[]{:S(2)}) copy-start(s32[8]{0:T(128)} %lengths.1) | copy-start | bytes 100
  5.2 24.6 %copy-start.7 = (bf16[512]{0:T(512)(128)(2,1)S(1)}, bf16[512]{0:T(512)(128)(2,1)}, u32[]{:S(2)}) copy-start(bf16[512]{0:T(512)(128)(2,1)} %param.19) | copy-start | bytes 3076
  5.2 24.7 %copy-start.8 = (bf16[512]{0:T(512)(128)(2,1)S(1)}, bf16[512]{0:T(512)(128)(2,1)}, u32[]{:S(2)}) copy-start(bf16[512]{0:T(512)(128)(2,1)} %param.20) | copy-start | bytes 3076
  5.2 2.3 %collective-permute-start = (f32[4,2,16,1280]{3,2,1,0:T(8,128)S(1)}, f32[4,2,16,1280]{3,2,1,0:T(8,128)S(1)}, u32[]{:S(2)}, u32[]{:S(2)}) collective-permute-start(f32[4,2,16,1280]{3,2,1,0:T(8,128)S(1)} %get-tuple-element.30), channel_id=1, source_target_pairs={{0,1},{1,0},{2,3},{3,2},{4,5},{5,4},{6,7},{7,6},{8,9},{9,8},{10,11... | collective-permute-start | bytes 1966088 | tf_op jit(solution)/shard_map/ppermute | solution.py:641
  7.5 57.8 %slice-start = ((s8[8388608]{0:T(1024)(128)(4,1)}), s8[4194304]{0:T(1024)(128)(4,1)S(1)}, s32[]{:S(2)}) async-start(s8[8388608]{0:T(1024)(128)(4,1)} %bitcast.8), calls=%async_computation | async-start | bytes 8388608
  7.6 29.0 %collective-permute-start.10 = (bf16[2,1024,512]{2,1,0:T(8,128)(2,1)S(1)}, bf16[2,1024,512]{2,1,0:T(8,128)(2,1)S(1)}, u32[]{:S(2)}, u32[]{:S(2)}) collective-permute-start(bf16[2,1024,512]{2,1,0:T(8,128)(2,1)S(1)} %copy-done.1), channel_id=1, source_target_pairs={{0,1},{1,0},{2,3},{3,2},{4,5},{5,4},{6,7},{7,6},{8,9},{9,8},{10,11... | collective-permute-start | bytes 6291464 | tf_op jit(solution)/shard_map/ppermute | solution.py:641
  8.0 30.2 %collective-permute-start.9 = (bf16[2,1024,512]{2,1,0:T(8,128)(2,1)S(1)}, bf16[2,1024,512]{2,1,0:T(8,128)(2,1)S(1)}, u32[]{:S(2)}, u32[]{:S(2)}) collective-permute-start(bf16[2,1024,512]{2,1,0:T(8,128)(2,1)S(1)} %copy-done), channel_id=1, source_target_pairs={{0,1},{1,0},{2,3},{3,2},{4,5},{5,4},{6,7},{7,6},{8,9},{9,8},{10,11... | collective-permute-start | bytes 6291464 | tf_op jit(solution)/shard_map/ppermute | solution.py:641
  8.2 36.2 %collective-permute-start.7 = (bf16[2,512,512]{2,1,0:T(8,128)(2,1)S(1)}, bf16[2,512,512]{2,1,0:T(8,128)(2,1)S(1)}, u32[]{:S(2)}, u32[]{:S(2)}) collective-permute-start(bf16[2,512,512]{2,1,0:T(8,128)(2,1)S(1)} %copy-done.2), channel_id=1, source_target_pairs={{0,1},{1,0},{2,3},{3,2},{4,5},{5,4},{6,7},{7,6},{8,9},{9,8},{10,11... | collective-permute-start | bytes 3145736 | tf_op jit(solution)/shard_map/ppermute | solution.py:641
  8.5 35.8 %collective-permute-start.8 = (bf16[2,512,512]{2,1,0:T(8,128)(2,1)S(1)}, bf16[2,512,512]{2,1,0:T(8,128)(2,1)S(1)}, u32[]{:S(2)}, u32[]{:S(2)}) collective-permute-start(bf16[2,512,512]{2,1,0:T(8,128)(2,1)S(1)} %copy-done.3), channel_id=1, source_target_pairs={{0,1},{1,0},{2,3},{3,2},{4,5},{5,4},{6,7},{7,6},{8,9},{9,8},{10,11... | collective-permute-start | bytes 3145736 | tf_op jit(solution)/shard_map/ppermute | solution.py:641
  8.7 7.4 %collective-permute-start.1 = (f32[2,16,1280]{2,1,0:T(8,128)S(1)}, f32[2,16,1280]{2,1,0:T(8,128)S(1)}, u32[]{:S(2)}, u32[]{:S(2)}) collective-permute-start(f32[2,16,1280]{2,1,0:T(8,128)S(1)} %get-tuple-element.55), channel_id=1, source_target_pairs={{0,4},{4,0},{8,12},{12,8},{1,5},{5,1},{9,13},{13,9},{2,6},{6,2},{1... | collective-permute-start | bytes 491528 | tf_op jit(solution)/shard_map/ppermute | solution.py:644
  16.1 10.1 %collective-permute-start.2 = (f32[2,16,1280]{2,1,0:T(8,128)S(1)}, f32[2,16,1280]{2,1,0:T(8,128)S(1)}, u32[]{:S(2)}, u32[]{:S(2)}) collective-permute-start(f32[2,16,1280]{2,1,0:T(8,128)S(1)} %get-tuple-element.54), channel_id=1, source_target_pairs={{0,8},{4,12},{8,0},{12,4},{1,9},{5,13},{9,1},{13,5},{2,10},{6,14},... | collective-permute-start | bytes 491528 | tf_op jit(solution)/shard_map/ppermute | solution.py:644
  26.2 7.9 %collective-permute-start.3 = (f32[2,16,1280]{2,1,0:T(8,128)S(1)}, f32[2,16,1280]{2,1,0:T(8,128)S(1)}, u32[]{:S(2)}, u32[]{:S(2)}) collective-permute-start(f32[2,16,1280]{2,1,0:T(8,128)S(1)} %get-tuple-element.53), channel_id=1, source_target_pairs={{0,12},{4,8},{8,4},{12,0},{1,13},{5,9},{9,5},{13,1},{2,14},{6,10},... | collective-permute-start | bytes 491528 | tf_op jit(solution)/shard_map/ppermute | solution.py:644
  34.2 7.5 %collective-permute-start.4 = (bf16[2,2,64,128]{3,2,1,0:T(8,128)(2,1)S(1)}, bf16[2,2,64,128]{3,2,1,0:T(8,128)(2,1)S(1)}, u32[]{:S(2)}, u32[]{:S(2)}) collective-permute-start(bf16[2,2,64,128]{3,2,1,0:T(8,128)(2,1)S(1)} %get-tuple-element.35.q_ref.refs_0_), channel_id=1, source_target_pairs={{0,4},{4,0},{8,12},{12,8},{1,5},{5,1},{9,13},{13,9},{2,6},{6,2},{1... | collective-permute-start | bytes 196616 | tf_op jit(solution)/shard_map/ppermute | solution.py:644
  36.6 6.4 %collective-permute-start.5 = (bf16[2,2,64,128]{3,2,1,0:T(8,128)(2,1)S(1)}, bf16[2,2,64,128]{3,2,1,0:T(8,128)(2,1)S(1)}, u32[]{:S(2)}, u32[]{:S(2)}) collective-permute-start(bf16[2,2,64,128]{3,2,1,0:T(8,128)(2,1)S(1)} %get-tuple-element.35.q_ref.refs_0_), channel_id=1, source_target_pairs={{0,8},{4,12},{8,0},{12,4},{1,9},{5,13},{9,1},{13,5},{2,10},{6,14},... | collective-permute-start | bytes 196616 | tf_op jit(solution)/shard_map/ppermute | solution.py:644
  38.3 6.1 %collective-permute-start.6 = (bf16[2,2,64,128]{3,2,1,0:T(8,128)(2,1)S(1)}, bf16[2,2,64,128]{3,2,1,0:T(8,128)(2,1)S(1)}, u32[]{:S(2)}, u32[]{:S(2)}) collective-permute-start(bf16[2,2,64,128]{3,2,1,0:T(8,128)(2,1)S(1)} %get-tuple-element.35.q_ref.refs_0_), channel_id=1, source_target_pairs={{0,12},{4,8},{8,4},{12,0},{1,13},{5,9},{9,5},{13,1},{2,14},{6,10},... | collective-permute-start | bytes 196616 | tf_op jit(solution)/shard_map/ppermute | solution.py:644
  39.0 5.3 %copy-start.5 = (s32[8]{0:T(128)S(1)}, s32[8]{0:T(128)}, u32[]{:S(2)}) copy-start(s32[8]{0:T(128)} %prompts.1) | copy-start | bytes 100
  39.0 26.2 %slice-start.1 = ((s8[8388608]{0:T(1024)(128)(4,1)}), s8[4194304]{0:T(1024)(128)(4,1)S(1)}, s32[]{:S(2)}) async-start(s8[8388608]{0:T(1024)(128)(4,1)} %bitcast.8), calls=%async_computation.1 | async-start | bytes 8388608
  47.3 4.6 %collective-permute-start.11 = (bf16[320,128]{1,0:T(8,128)(2,1)S(1)}, bf16[320,128]{1,0:T(8,128)(2,1)S(1)}, u32[]{:S(2)}, u32[]{:S(2)}) collective-permute-start(bf16[320,128]{1,0:T(8,128)(2,1)S(1)} %get-tuple-element.48), channel_id=1, source_target_pairs={{0,4},{4,0},{8,12},{12,8},{1,5},{5,1},{9,13},{13,9},{2,6},{6,2},{1... | collective-permute-start | bytes 245768 | tf_op jit(solution)/shard_map/ppermute | solution.py:644
  47.3 8.3 %collective-permute-start.12 = (bf16[320,128]{1,0:T(8,128)(2,1)S(1)}, bf16[320,128]{1,0:T(8,128)(2,1)S(1)}, u32[]{:S(2)}, u32[]{:S(2)}) collective-permute-start(bf16[320,128]{1,0:T(8,128)(2,1)S(1)} %get-tuple-element.49), channel_id=1, source_target_pairs={{0,8},{4,12},{8,0},{12,4},{1,9},{5,13},{9,1},{13,5},{2,10},{6,14},... | collective-permute-start | bytes 245768 | tf_op jit(solution)/shard_map/ppermute | solution.py:644
  49.3 6.4 %collective-permute-start.13 = (bf16[320,128]{1,0:T(8,128)(2,1)S(1)}, bf16[320,128]{1,0:T(8,128)(2,1)S(1)}, u32[]{:S(2)}, u32[]{:S(2)}) collective-permute-start(bf16[320,128]{1,0:T(8,128)(2,1)S(1)} %get-tuple-element.50), channel_id=1, source_target_pairs={{0,12},{4,8},{8,4},{12,0},{1,13},{5,9},{9,5},{13,1},{2,14},{6,10},... | collective-permute-start | bytes 245768 | tf_op jit(solution)/shard_map/ppermute | solution.py:644
  56.0 4.5 %collective-permute-start.15 = (bf16[16,2048]{1,0:T(8,128)(2,1)S(1)}, bf16[16,2048]{1,0:T(8,128)(2,1)S(1)}, u32[]{:S(2)}, u32[]{:S(2)}) collective-permute-start(bf16[16,2048]{1,0:T(8,128)(2,1)S(1)} %merge.1.refs_0_), channel_id=1, source_target_pairs={{0,4},{4,0},{8,12},{12,8},{1,5},{5,1},{9,13},{13,9},{2,6},{6,2},{1... | collective-permute-start | bytes 196616 | tf_op jit(solution)/shard_map/ppermute | solution.py:644
  57.5 6.6 %collective-permute-start.17 = (bf16[16,2048]{1,0:T(8,128)(2,1)S(1)}, bf16[16,2048]{1,0:T(8,128)(2,1)S(1)}, u32[]{:S(2)}, u32[]{:S(2)}) collective-permute-start(bf16[16,2048]{1,0:T(8,128)(2,1)S(1)} %merge.1.refs_0_), channel_id=1, source_target_pairs={{0,8},{4,12},{8,0},{12,4},{1,9},{5,13},{9,1},{13,5},{2,10},{6,14},... | collective-permute-start | bytes 196616 | tf_op jit(solution)/shard_map/ppermute | solution.py:644
  59.1 6.2 %collective-permute-start.19 = (bf16[16,2048]{1,0:T(8,128)(2,1)S(1)}, bf16[16,2048]{1,0:T(8,128)(2,1)S(1)}, u32[]{:S(2)}, u32[]{:S(2)}) collective-permute-start(bf16[16,2048]{1,0:T(8,128)(2,1)S(1)} %merge.1.refs_0_), channel_id=1, source_target_pairs={{0,12},{4,8},{8,4},{12,0},{1,13},{5,9},{9,5},{13,1},{2,14},{6,10},... | collective-permute-start | bytes 196616 | tf_op jit(solution)/shard_map/ppermute | solution.py:644
  60.5 5.7 %collective-permute-start.14 = (bf16[16,2048]{1,0:T(8,128)(2,1)S(1)}, bf16[16,2048]{1,0:T(8,128)(2,1)S(1)}, u32[]{:S(2)}, u32[]{:S(2)}) collective-permute-start(bf16[16,2048]{1,0:T(8,128)(2,1)S(1)} %merge.1.refs_0_), channel_id=1, source_target_pairs={{0,1},{1,0},{2,3},{3,2},{4,5},{5,4},{6,7},{7,6},{8,9},{9,8},{10,11... | collective-permute-start | bytes 196616 | tf_op jit(solution)/shard_map/ppermute | solution.py:641
  60.5 5.7 %collective-permute-start.16 = (bf16[16,2048]{1,0:T(8,128)(2,1)S(1)}, bf16[16,2048]{1,0:T(8,128)(2,1)S(1)}, u32[]{:S(2)}, u32[]{:S(2)}) collective-permute-start(bf16[16,2048]{1,0:T(8,128)(2,1)S(1)} %collective-permute-done.15.refs_1_), channel_id=1, source_target_pairs={{0,1},{1,0},{2,3},{3,2},{4,5},{5,4},{6,7},{7,6},{8,9},{9,8},{10,11... | collective-permute-start | bytes 196616 | tf_op jit(solution)/shard_map/ppermute | solution.py:641
  64.1 2.0 %collective-permute-start.18 = (bf16[16,2048]{1,0:T(8,128)(2,1)S(1)}, bf16[16,2048]{1,0:T(8,128)(2,1)S(1)}, u32[]{:S(2)}, u32[]{:S(2)}) collective-permute-start(bf16[16,2048]{1,0:T(8,128)(2,1)S(1)} %collective-permute-done.17.refs_2_), channel_id=1, source_target_pairs={{0,1},{1,0},{2,3},{3,2},{4,5},{5,4},{6,7},{7,6},{8,9},{9,8},{10,11... | collective-permute-start | bytes 196616 | tf_op jit(solution)/shard_map/ppermute | solution.py:641
  65.2 1.3 %collective-permute-start.20 = (bf16[16,2048]{1,0:T(8,128)(2,1)S(1)}, bf16[16,2048]{1,0:T(8,128)(2,1)S(1)}, u32[]{:S(2)}, u32[]{:S(2)}) collective-permute-start(bf16[16,2048]{1,0:T(8,128)(2,1)S(1)} %collective-permute-done.19.refs_3_), channel_id=1, source_target_pairs={{0,1},{1,0},{2,3},{3,2},{4,5},{5,4},{6,7},{7,6},{8,9},{9,8},{10,11... | collective-permute-start | bytes 196616 | tf_op jit(solution)/shard_map/ppermute | solution.py:641
  67.4 4.3 %collective-permute-start.21 = (bf16[32,1024]{1,0:T(8,128)(2,1)S(1)}, bf16[32,1024]{1,0:T(8,128)(2,1)S(1)}, u32[]{:S(2)}, u32[]{:S(2)}) collective-permute-start(bf16[32,1024]{1,0:T(8,128)(2,1)S(1)} %get-tuple-element.52), channel_id=1, source_target_pairs={{0,2},{2,0},{1,3},{3,1},{4,6},{6,4},{5,7},{7,5},{8,10},{10,8},{9,1... | collective-permute-start | bytes 196616 | tf_op jit(solution)/shard_map/ppermute | solution.py:688

commit v2 on v1

--- a/solution.py
+++ b/solution.py
@@ -354,6 +354,37 @@
     )(*sums, *biases, cosine, sine)
 
 
+def fetch_kernel(*refs):
+    count = len(refs) // 2
+    sems = refs[-1]
+    seq = lax.axis_index("seq")
+    copies = []
+    for n, (source, target) in enumerate(zip(refs[:count], refs[count:-1])):
+        cols = target.shape[2]
+        part = source.at[:, :, pl.ds(pl.multiple_of(seq * cols, cols), cols)]
+        copies.append(pltpu.make_async_copy(part, target, sems.at[n]))
+    for copy in copies:
+        copy.start()
+    for copy in copies:
+        copy.wait()
+
+
+def fetch(caches):
+    shapes = [(c.shape[0], c.shape[1], c.shape[2] // 2) for c in caches]
+    return pl.pallas_call(
+        fetch_kernel,
+        in_specs=[pl.BlockSpec(memory_space=pltpu.HBM)] * len(caches),
+        out_specs=[pl.BlockSpec(memory_space=pltpu.VMEM)] * len(caches),
+        out_shape=[jax.ShapeDtypeStruct(s, jnp.bfloat16) for s in shapes],
+        scratch_shapes=[pltpu.SemaphoreType.DMA((len(caches),))],
+        compiler_params=pltpu.CompilerParams(vmem_limit_bytes=1 << 20),
+        cost_estimate=pl.CostEstimate(
+            flops=0, bytes_accessed=2 * sum(math.prod(s) for s in shapes), transcendentals=0
+        ),
+        name="fetch",
+    )(*[pltpu.with_memory_space_constraint(c, pltpu.HBM) for c in caches])
+
+
 def own_kernel(scale, guess, lengths, q_ref, kn_ref, vn_ref, k0_ref, k1_ref, v0_ref, v1_ref, n_ref, m_ref, l_ref):
     per, kh, width, _ = q_ref.shape
     span = k0_ref.shape[1]
@@ -371,8 +402,9 @@
         for j in range(kh):
             q = q_ref[i, j]
             at = pl.ds(pl.multiple_of((seq * kh + j) * HD, HD), HD)
-            keys = (k0_ref[i, :, at], k1_ref[i, :, at], kn_ref[j])
-            values = (v0_ref[i, :, at], v1_ref[i, :, at], vn_ref[j])
+            mine = slice(j * HD, (j + 1) * HD)
+            keys = (k0_ref[i, :, mine], k1_ref[i, :, at], kn_ref[j])
+            values = (v0_ref[i, :, mine], v1_ref[i, :, at], vn_ref[j])
             scores = [jnp.where(see, contract_last(q, k), NEG_FILL) for k, see in zip(keys, sees)]
             peak = jnp.max(scores[0], axis=1, keepdims=True)
             for s in scores[1:]:
@@ -447,25 +479,26 @@
         for j in range(kh):
             at = pl.ds(pl.multiple_of((seq * kh + j) * HD, HD), HD)
             q = jnp.concatenate([q_all[n, j] for n in ids], axis=0)
-            scores = [contract_last(q, k_ref[p, :, at]) for k_ref in (k0_ref, k1_ref)]
+            mine = slice(j * HD, (j + 1) * HD)
+            scores = [contract_last(q, k_ref[p, :, to]) for k_ref, to in ((k0_ref, mine), (k1_ref, at))]
             peak = jnp.maximum(
                 jnp.max(scores[0], axis=1, keepdims=True), jnp.max(scores[1], axis=1, keepdims=True)
             )
             total = jnp.zeros(peak.shape, jnp.float32)
             numer = jnp.zeros((share * width, HD), jnp.float32)
-            for s, v_ref in zip(scores, (v0_ref, v1_ref)):
+            for s, v_ref, to in zip(scores, (v0_ref, v1_ref), (mine, at)):
                 w = jnp.exp2((s - peak) * (scale * LOG2E))
                 total = total + jnp.sum(w, axis=1, keepdims=True)
                 numer = numer + jnp.dot(
-                    w.astype(jnp.bfloat16), v_ref[p, :, at], preferred_element_type=jnp.float32
+                    w.astype(jnp.bfloat16), v_ref[p, :, to], preferred_element_type=jnp.float32
                 )
             peak = jnp.broadcast_to(peak * scale, numer.shape)
             total = jnp.broadcast_to(total, numer.shape)
-            for n, to in enumerate(ids):
+            for n, slot in enumerate(ids):
                 span = slice(n * width, (n + 1) * width)
-                n_all[to, j] = numer[span]
-                m_all[to, j] = peak[span]
-                l_all[to, j] = total[span]
+                n_all[slot, j] = numer[span]
+                m_all[slot, j] = peak[span]
+                l_all[slot, j] = total[span]
 
     for i in range(per):
         for h in range(kh):
@@ -650,7 +683,12 @@
     send, keep = project(hidden, w_query, w_key, w_value, roll, kh)
     got = across(send)
     terms = [keep[k] + got[k] for k in range(roll)]
-    sums = [terms[0]] + hops(lambda k: terms[k])
+    if roll == 4:
+        relayed = hop(terms[3], 1)
+        near = hop(terms[1], 1)
+        sums = [terms[0], near, hop(terms[2] + relayed, 2)]
+    else:
+        sums = [terms[0]] + hops(lambda k: terms[k])
     caches = (suffix_keys, suffix_values, prefix_keys, prefix_values)
     _, small = lax.optimization_barrier(
         (terms[0], (suffix_lengths, b_query, b_key, b_value, *caches))
@@ -658,6 +696,7 @@
     caches = small[4:]
 
     sk_got, sv_got, pk_got, pv_got = [across(x) for x in caches]
+    sk_own, sv_own, pk_own, pv_own = fetch(caches)
 
     row_ids = jnp.arange(hidden.shape[0], dtype=jnp.int32)
     prefix_total = prefix_keys.shape[1] * roll * 2
@@ -675,10 +714,10 @@
     q, k_new, v_new = finish(sums, biases, cosine, sine, per)
     queries = [q] + hops(lambda k: q)
     own = own_attention(
-        suffix_lengths, q, k_new, v_new, suffix_keys, sk_got, suffix_values, sv_got, scale, guess
+        suffix_lengths, q, k_new, v_new, sk_own, sk_got, sv_own, sv_got, scale, guess
     )
     own, packed = prefix_attention(
-        prompt_of, queries, prefix_keys, pk_got, prefix_values, pv_got, own, scale
+        prompt_of, queries, pk_own, pk_got, pv_own, pv_got, own, scale
     )
     packed = hops(lambda k: packed[k - 1])
     share = merge(own, packed, group)

time: 72.5 us -> 68.5 us (0.945)
  waiting for transfers between devices: 31.6 us -> 27.8 us
  starting transfers between devices: 26.5 us -> 24.2 us
  Pallas kernels: 12.8 us -> 14.8 us
    ppermute x12, waiting for transfers between devices: 26.7 us -> 23 us  [hop(): return lax.ppermute(x, 'roll', [(n, n ^ k) for n in range(roll)])]
    ppermute x12, starting transfers between devices: 22.8 us -> 20.5 us  [hop(): return lax.ppermute(x, 'roll', [(n, n ^ k) for n in range(roll)])]
    pallas_call x0 -> x1, Pallas kernels: none -> 2.01 us  [fetch(): pl.pallas_call(fetch_kernel, in_specs=[pl.BlockSpec(memory_space=pltpu.HB...]
  transfers between devices with their start and end apart: 22 -> 22, of which waited for: 12 -> 12; matrix products, arithmetic and copies ran while one was open for 1% -> 1% of each run, Pallas kernels for 5% -> 8%
where the time goes in v2:
time: 68.5 us; the launch traced here: 68.3 us
  waiting for transfers between devices  27.8 us (41%)
  starting transfers between devices  24.2 us (35%)
  Pallas kernels  14.8 us (22%)
  other arithmetic  1.13 us (2%)
    ppermute x12, waiting for transfers between devices, hop(): return lax.ppermute(x, 'roll', [(n, n ^ k) for n in range(roll)])  23 us
    ppermute x12, starting transfers between devices, hop(): return lax.ppermute(x, 'roll', [(n, n ^ k) for n in range(roll)])  20.5 us
    pallas_call x1, Pallas kernels, project(): pl.pallas_call(project_kernel, out_shape=[out, out], in_specs=[hbm] * 4,...  5.13 us
    pallas_call x1, Pallas kernels, prefix_attention(): pl.pallas_call(functools.partial(prefix_kernel, scale, roll), in_specs=[p...  2.84 us
    ppermute x1, waiting for transfers between devices, fast_body(): arrived = lax.ppermute(sent, 'tp', [(0, 1), (1, 0)])  2.79 us
    pallas_call x1, Pallas kernels, own_attention(): pl.pallas_call(functools.partial(own_kernel, scale, guess), in_specs=[pl....  2.6 us
    ppermute x9, starting transfers between devices, across(): return lax.ppermute(x, 'seq', [(0, 1), (1, 0)])  2.2 us
    ppermute x9, waiting for transfers between devices, across(): return lax.ppermute(x, 'seq', [(0, 1), (1, 0)])  2.09 us
  transfers between devices with their start and end apart: 22, of which 12 were waited for; matrix products, arithmetic and copies ran while one was open for 1% of the time, Pallas kernels for 8%

profile of v2, /device:TPU:0, one launch (start us, length us, event | category | flops | bytes accessed | tf_op | source)
XLA Modules:
  0.0 68.3 jit_solution(13895561236136561766)
XLA Ops:
  0.0 5.1 %project.1 = (f32[4,2,16,1280]{3,2,1,0:T(8,128)S(1)}, f32[4,2,16,1280]{3,2,1,0:T(8,128)S(1)}) custom-call(bf16[64,1024]{1,0:T(8,128)(2,1)} %x_ref.1, bf16[1024,4096]{1,0:T(8,128)(2,1)} %wq_ref.1, bf16[1024,512]{1,0:T(8,128)(2,1)} %wk_ref.1, bf16[1024,512]{1,0:T(8,128)(2,1)} %wv_ref.1), custom_call_target="tpu_custom_call" | custom-call | flops 671088640 | bytes 10485760 | tf_op jit(solution)/shard_map/project/pallas_call | solution.py:282
  5.1 0.0 copy-start.6
  5.2 0.0 copy-start.7
  5.2 0.0 copy-start.8
  5.2 0.6 collective-permute-start
  5.8 1.7 %collective-permute-done = f32[4,2,16,1280]{3,2,1,0:T(8,128)S(1)} collective-permute-done((f32[4,2,16,1280]{3,2,1,0:T(8,128)S(1)}, f32[4,2,16,1280]{3,2,1,0:T(8,128)S(1)}, u32[]{:S(2)}, u32[]{:S(2)}) %collective-permute-start) | collective-permute-done | bytes 655392 | tf_op jit(solution)/shard_map/ppermute | solution.py:674
  7.5 0.1 fusion
  7.6 0.4 collective-permute-start.10
  8.0 0.1 collective-permute-start.9
  8.2 2.9 %collective-permute-start.2 = (f32[2,16,1280]{2,1,0:T(8,128)S(1)}, f32[2,16,1280]{2,1,0:T(8,128)S(1)}, u32[]{:S(2)}, u32[]{:S(2)}) collective-permute-start(f32[2,16,1280]{2,1,0:T(8,128)S(1)} %get-tuple-element.61), channel_id=1, source_target_pairs={{0,4},{4,0},{8,12},{12,8},{1,5},{5,1},{9,13},{13,9},{2,6},{6,2},{1... | collective-permute-start | bytes 491528 | tf_op jit(solution)/shard_map/ppermute | solution.py:677
  11.1 0.5 collective-permute-start.8
  11.6 0.1 select_reduce_fusion
  11.7 3.9 %collective-permute-done.2 = f32[2,16,1280]{2,1,0:T(8,128)S(1)} collective-permute-done((f32[2,16,1280]{2,1,0:T(8,128)S(1)}, f32[2,16,1280]{2,1,0:T(8,128)S(1)}, u32[]{:S(2)}, u32[]{:S(2)}) %collective-permute-start.2) | collective-permute-done | bytes 163872 | tf_op jit(solution)/shard_map/ppermute | solution.py:677
  15.6 1.7 %collective-permute-start.1 = (f32[2,16,1280]{2,1,0:T(8,128)S(1)}, f32[2,16,1280]{2,1,0:T(8,128)S(1)}, u32[]{:S(2)}, u32[]{:S(2)}) collective-permute-start(f32[2,16,1280]{2,1,0:T(8,128)S(1)} %get-tuple-element.62), channel_id=1, source_target_pairs={{0,4},{4,0},{8,12},{12,8},{1,5},{5,1},{9,13},{13,9},{2,6},{6,2},{1... | collective-permute-start | bytes 491528 | tf_op jit(solution)/shard_map/ppermute | solution.py:677
  17.4 3.9 %collective-permute-done.1.refs_1_ = f32[2,16,1280]{2,1,0:T(8,128)S(1)} collective-permute-done((f32[2,16,1280]{2,1,0:T(8,128)S(1)}, f32[2,16,1280]{2,1,0:T(8,128)S(1)}, u32[]{:S(2)}, u32[]{:S(2)}) %collective-permute-start.1) | collective-permute-done | bytes 163872 | tf_op jit(solution)/shard_map/ppermute | solution.py:677
  21.3 2.5 %collective-permute-start.3 = (f32[2,16,1280]{2,1,0:T(8,128)S(1)}, f32[2,16,1280]{2,1,0:T(8,128)S(1)}, u32[]{:S(2)}, u32[]{:S(2)}) collective-permute-start(f32[2,16,1280]{2,1,0:T(8,128)S(1)} %fusion.2), channel_id=1, source_target_pairs={{0,8},{4,12},{8,0},{12,4},{1,9},{5,13},{9,1},{13,5},{2,10},{6,14},... | collective-permute-start | bytes 491528 | tf_op jit(solution)/shard_map/ppermute | solution.py:677
  23.8 0.2 fusion.5
  24.1 0.1 pad_maximum_fusion
  24.2 6.4 %collective-permute-done.3.refs_2_ = f32[2,16,1280]{2,1,0:T(8,128)S(1)} collective-permute-done((f32[2,16,1280]{2,1,0:T(8,128)S(1)}, f32[2,16,1280]{2,1,0:T(8,128)S(1)}, u32[]{:S(2)}, u32[]{:S(2)}) %collective-permute-start.3) | collective-permute-done | bytes 163872 | tf_op jit(solution)/shard_map/ppermute | solution.py:677
  30.6 0.1 finish.1
  30.7 0.3 collective-permute-start.4
  31.0 3.4 %collective-permute-start.5 = (bf16[2,2,64,128]{3,2,1,0:T(8,128)(2,1)S(1)}, bf16[2,2,64,128]{3,2,1,0:T(8,128)(2,1)S(1)}, u32[]{:S(2)}, u32[]{:S(2)}) collective-permute-start(bf16[2,2,64,128]{3,2,1,0:T(8,128)(2,1)S(1)} %get-tuple-element.39.q_ref.refs_0_), channel_id=1, source_target_pairs={{0,8},{4,12},{8,0},{12,4},{1,9},{5,13},{9,1},{13,5},{2,10},{6,14},... | collective-permute-start | bytes 196616 | tf_op jit(solution)/shard_map/ppermute | solution.py:677
  34.4 0.7 %collective-permute-start.6 = (bf16[2,2,64,128]{3,2,1,0:T(8,128)(2,1)S(1)}, bf16[2,2,64,128]{3,2,1,0:T(8,128)(2,1)S(1)}, u32[]{:S(2)}, u32[]{:S(2)}) collective-permute-start(bf16[2,2,64,128]{3,2,1,0:T(8,128)(2,1)S(1)} %get-tuple-element.39.q_ref.refs_0_), channel_id=1, source_target_pairs={{0,12},{4,8},{8,4},{12,0},{1,13},{5,9},{9,5},{13,1},{2,14},{6,10},... | collective-permute-start | bytes 196616 | tf_op jit(solution)/shard_map/ppermute | solution.py:677
  35.2 2.0 %fetch.1 = (bf16[2,1024,256]{2,1,0:T(8,128)(2,1)S(1)}, bf16[2,1024,256]{2,1,0:T(8,128)(2,1)S(1)}, bf16[2,512,256]{2,1,0:T(8,128)(2,1)S(1)}, bf16[2,512,256]{2,1,0:T(8,128)(2,1)S(1)}) custom-call(bf16[2,1024,512]{2,1,0:T(8,128)(2,1)} %refs_0_, bf16[2,1024,512]{2,1,0:T(8,128)(2,1)} %refs_1_, bf16[2,512,512]{2,1,0:T(8,128)(2,1)} %refs_2_, ...), custom_call_target="tpu_custom_call" | custom-call | bytes 3145728 | tf_op jit(solution)/shard_map/fetch/pallas_call | solution.py:374
  37.2 0.0 copy-start.1
  37.2 0.0 slice-start.1
  37.2 2.6 %own_attention.1 = (f32[2,2,64,128]{3,2,1,0:T(8,128)S(1)}, f32[2,2,64,128]{3,2,1,0:T(8,128)S(1)}, f32[2,2,64,128]{3,2,1,0:T(8,128)S(1)}) custom-call(s32[8]{0:T(128)S(1)} %copy-done, bf16[2,2,64,128]{3,2,1,0:T(8,128)(2,1)S(1)} %get-tuple-element.39.q_ref.refs_0_, bf16[2,16,128]{2,1,0:T(8,128)(2,1)S(1)} %get-tuple-element.46.kn_ref, ...), custom_call_target="tpu_custom_call" | custom-call | flops 268435456 | bytes 4194304 | tf_op jit(solution)/shard_map/own_attention/pallas_call | solution.py:430
  39.9 0.6 collective-permute-done.6.refs_3_
  40.5 2.8 %prefix_attention.1 = (f32[2,2,64,128]{3,2,1,0:T(8,128)S(1)}, f32[2,2,64,128]{3,2,1,0:T(8,128)S(1)}, f32[2,2,64,128]{3,2,1,0:T(8,128)S(1)}, bf16[320,128]{1,0:T(...) custom-call(s32[8]{0:T(128)S(1)} %copy-done.1, ...), custom_call_target="tpu_custom_call" | custom-call | flops 536870912 | bytes 2097152 | tf_op jit(solution)/shard_map/prefix_attention/pallas_call | solution.py:534
  43.3 0.1 collective-permute-start.11
  43.4 3.0 %collective-permute-start.12 = (bf16[320,128]{1,0:T(8,128)(2,1)S(1)}, bf16[320,128]{1,0:T(8,128)(2,1)S(1)}, u32[]{:S(2)}, u32[]{:S(2)}) collective-permute-start(bf16[320,128]{1,0:T(8,128)(2,1)S(1)} %get-tuple-element.57), channel_id=1, source_target_pairs={{0,8},{4,12},{8,0},{12,4},{1,9},{5,13},{9,1},{13,5},{2,10},{6,14},... | collective-permute-start | bytes 245768 | tf_op jit(solution)/shard_map/ppermute | solution.py:677
  46.5 1.3 %collective-permute-start.13 = (bf16[320,128]{1,0:T(8,128)(2,1)S(1)}, bf16[320,128]{1,0:T(8,128)(2,1)S(1)}, u32[]{:S(2)}, u32[]{:S(2)}) collective-permute-start(bf16[320,128]{1,0:T(8,128)(2,1)S(1)} %get-tuple-element.58), channel_id=1, source_target_pairs={{0,12},{4,8},{8,4},{12,0},{1,13},{5,9},{9,5},{13,1},{2,14},{6,10},... | collective-permute-start | bytes 245768 | tf_op jit(solution)/shard_map/ppermute | solution.py:677
  47.8 0.2 collective-permute-done.11.refs_0_
  48.0 2.7 %collective-permute-done.12.refs_1_ = bf16[320,128]{1,0:T(8,128)(2,1)S(1)} collective-permute-done((bf16[320,128]{1,0:T(8,128)(2,1)S(1)}, bf16[320,128]{1,0:T(8,128)(2,1)S(1)}, u32[]{:S(2)}, u32[]{:S(2)}) %collective-permute-start.12) | collective-permute-done | bytes 81952 | tf_op jit(solution)/shard_map/ppermute | solution.py:677
  50.7 2.1 %collective-permute-done.13.refs_2_ = bf16[320,128]{1,0:T(8,128)(2,1)S(1)} collective-permute-done((bf16[320,128]{1,0:T(8,128)(2,1)S(1)}, bf16[320,128]{1,0:T(8,128)(2,1)S(1)}, u32[]{:S(2)}, u32[]{:S(2)}) %collective-permute-start.13) | collective-permute-done | bytes 81952 | tf_op jit(solution)/shard_map/ppermute | solution.py:677
  52.8 0.4 merge.1.refs_0_
  53.1 0.1 collective-permute-start.15
  53.2 1.9 %collective-permute-start.17 = (bf16[16,2048]{1,0:T(8,128)(2,1)S(1)}, bf16[16,2048]{1,0:T(8,128)(2,1)S(1)}, u32[]{:S(2)}, u32[]{:S(2)}) collective-permute-start(bf16[16,2048]{1,0:T(8,128)(2,1)S(1)} %merge.1.refs_0_), channel_id=1, source_target_pairs={{0,8},{4,12},{8,0},{12,4},{1,9},{5,13},{9,1},{13,5},{2,10},{6,14},... | collective-permute-start | bytes 196616 | tf_op jit(solution)/shard_map/ppermute | solution.py:677
  55.1 2.4 %collective-permute-start.19 = (bf16[16,2048]{1,0:T(8,128)(2,1)S(1)}, bf16[16,2048]{1,0:T(8,128)(2,1)S(1)}, u32[]{:S(2)}, u32[]{:S(2)}) collective-permute-start(bf16[16,2048]{1,0:T(8,128)(2,1)S(1)} %merge.1.refs_0_), channel_id=1, source_target_pairs={{0,12},{4,8},{8,4},{12,0},{1,13},{5,9},{9,5},{13,1},{2,14},{6,10},... | collective-permute-start | bytes 196616 | tf_op jit(solution)/shard_map/ppermute | solution.py:677
  57.6 0.5 collective-permute-start.16
  58.1 0.3 collective-permute-done.17.refs_2_
  58.4 2.8 %collective-permute-done.19.refs_3_ = bf16[16,2048]{1,0:T(8,128)(2,1)S(1)} collective-permute-done((bf16[16,2048]{1,0:T(8,128)(2,1)S(1)}, bf16[16,2048]{1,0:T(8,128)(2,1)S(1)}, u32[]{:S(2)}, u32[]{:S(2)}) %collective-permute-start.19) | collective-permute-done | bytes 65568 | tf_op jit(solution)/shard_map/ppermute | solution.py:677
  61.3 0.8 %output_mine.1.refs_5_ = f32[64,1024]{1,0:T(8,128)S(1)} custom-call(bf16[16,2048]{1,0:T(8,128)(2,1)S(1)} %merge.1.refs_0_, bf16[16,2048]{1,0:T(8,128)(2,1)S(1)} %collective-permute-done.15.refs_1_, bf16[16,2048]{1,0:T(8,128)(2,1)S(1)} %collective-permute-done.17.refs_2_, bf16[16,2048]{1,0:T(8,128)(2,1)S(1)} %collective-permute-done.19.refs_3_, ...), custom_call_target="tpu_custom_call" | custom-call | flops 268435456 | bytes 4194304 | tf_op jit(solution)/shard_map/output_mine/pallas_call | solution.py:634
  62.1 0.3 collective-permute-done.20.refs_3_
  62.5 0.8 %output_theirs.1 = (f32[32,1024]{1,0:T(8,128)S(1)}, bf16[32,1024]{1,0:T(8,128)(2,1)S(1)}) custom-call(bf16[16,2048]{1,0:T(8,128)(2,1)S(1)} %collective-permute-done.14.refs_0_, bf16[16,2048]{1,0:T(8,128)(2,1)S(1)} %collective-permute-done.16.refs_1_, bf16[16,2048]{1,0:T(8,128)(2,1)S(1)} %collective-permute-done.18.refs_2_, ...), custom_call_target="tpu_custom_call" | custom-call | flops 268435456 | bytes 4194304 | tf_op jit(solution)/shard_map/output_theirs/pallas_call | solution.py:634
  63.3 1.5 %collective-permute-start.21 = (bf16[32,1024]{1,0:T(8,128)(2,1)S(1)}, bf16[32,1024]{1,0:T(8,128)(2,1)S(1)}, u32[]{:S(2)}, u32[]{:S(2)}) collective-permute-start(bf16[32,1024]{1,0:T(8,128)(2,1)S(1)} %get-tuple-element.60), channel_id=1, source_target_pairs={{0,2},{2,0},{1,3},{3,1},{4,6},{6,4},{5,7},{7,5},{8,10},{10,8},{9,1... | collective-permute-start | bytes 196616 | tf_op jit(solution)/shard_map/ppermute | solution.py:727
  64.9 2.8 %collective-permute-done.21 = bf16[32,1024]{1,0:T(8,128)(2,1)S(1)} collective-permute-done((bf16[32,1024]{1,0:T(8,128)(2,1)S(1)}, bf16[32,1024]{1,0:T(8,128)(2,1)S(1)}, u32[]{:S(2)}, u32[]{:S(2)}) %collective-permute-start.21) | collective-permute-done | bytes 65568 | tf_op jit(solution)/shard_map/ppermute | solution.py:727
  67.7 0.6 add_convert_fusion
  (39 shorter events, 0.1 us)
Async XLA Ops:
  0.0 11.1 %copy-start.4 = (bf16[2,512,512]{2,1,0:T(8,128)(2,1)S(1)}, bf16[2,512,512]{2,1,0:T(8,128)(2,1)}, u32[]{:S(2)}) copy-start(bf16[2,512,512]{2,1,0:T(8,128)(2,1)} %refs_2_) | copy-start | bytes 3145732
  0.0 11.1 %copy-start.5 = (bf16[2,512,512]{2,1,0:T(8,128)(2,1)S(1)}, bf16[2,512,512]{2,1,0:T(8,128)(2,1)}, u32[]{:S(2)}) copy-start(bf16[2,512,512]{2,1,0:T(8,128)(2,1)} %refs_3_) | copy-start | bytes 3145732
  0.0 8.0 %copy-start.2 = (bf16[2,1024,512]{2,1,0:T(8,128)(2,1)S(1)}, bf16[2,1024,512]{2,1,0:T(8,128)(2,1)}, u32[]{:S(2)}) copy-start(bf16[2,1024,512]{2,1,0:T(8,128)(2,1)} %refs_0_) | copy-start | bytes 6291460
  0.0 7.6 %copy-start.3 = (bf16[2,1024,512]{2,1,0:T(8,128)(2,1)S(1)}, bf16[2,1024,512]{2,1,0:T(8,128)(2,1)}, u32[]{:S(2)}) copy-start(bf16[2,1024,512]{2,1,0:T(8,128)(2,1)} %refs_1_) | copy-start | bytes 6291460
  0.0 11.6 %copy-start = (s32[8]{0:T(128)S(1)}, s32[8]{0:T(128)}, u32[]{:S(2)}) copy-start(s32[8]{0:T(128)} %lengths.1) | copy-start | bytes 100
  5.1 18.8 %copy-start.6 = (bf16[4096]{0:T(1024)(128)(2,1)S(1)}, bf16[4096]{0:T(1024)(128)(2,1)}, u32[]{:S(2)}) copy-start(bf16[4096]{0:T(1024)(128)(2,1)} %param.18) | copy-start | bytes 24580
  5.2 18.9 %copy-start.7 = (bf16[512]{0:T(512)(128)(2,1)S(1)}, bf16[512]{0:T(512)(128)(2,1)}, u32[]{:S(2)}) copy-start(bf16[512]{0:T(512)(128)(2,1)} %param.19) | copy-start | bytes 3076
  5.2 18.9 %copy-start.8 = (bf16[512]{0:T(512)(128)(2,1)S(1)}, bf16[512]{0:T(512)(128)(2,1)}, u32[]{:S(2)}) copy-start(bf16[512]{0:T(512)(128)(2,1)} %param.20) | copy-start | bytes 3076
  5.2 2.3 %collective-permute-start = (f32[4,2,16,1280]{3,2,1,0:T(8,128)S(1)}, f32[4,2,16,1280]{3,2,1,0:T(8,128)S(1)}, u32[]{:S(2)}, u32[]{:S(2)}) collective-permute-start(f32[4,2,16,1280]{3,2,1,0:T(8,128)S(1)} %get-tuple-element.34), channel_id=1, source_target_pairs={{0,1},{1,0},{2,3},{3,2},{4,5},{5,4},{6,7},{7,6},{8,9},{9,8},{10,11... | collective-permute-start | bytes 1966088 | tf_op jit(solution)/shard_map/ppermute | solution.py:674
  7.6 23.4 %collective-permute-start.10 = (bf16[2,1024,512]{2,1,0:T(8,128)(2,1)S(1)}, bf16[2,1024,512]{2,1,0:T(8,128)(2,1)S(1)}, u32[]{:S(2)}, u32[]{:S(2)}) collective-permute-start(bf16[2,1024,512]{2,1,0:T(8,128)(2,1)S(1)} %copy-done.3), channel_id=1, source_target_pairs={{0,1},{1,0},{2,3},{3,2},{4,5},{5,4},{6,7},{7,6},{8,9},{9,8},{10,11... | collective-permute-start | bytes 6291464 | tf_op jit(solution)/shard_map/ppermute | solution.py:674
  8.0 26.4 %collective-permute-start.9 = (bf16[2,1024,512]{2,1,0:T(8,128)(2,1)S(1)}, bf16[2,1024,512]{2,1,0:T(8,128)(2,1)S(1)}, u32[]{:S(2)}, u32[]{:S(2)}) collective-permute-start(bf16[2,1024,512]{2,1,0:T(8,128)(2,1)S(1)} %copy-done.2), channel_id=1, source_target_pairs={{0,1},{1,0},{2,3},{3,2},{4,5},{5,4},{6,7},{7,6},{8,9},{9,8},{10,11... | collective-permute-start | bytes 6291464 | tf_op jit(solution)/shard_map/ppermute | solution.py:674
  8.2 7.5 %collective-permute-start.2 = (f32[2,16,1280]{2,1,0:T(8,128)S(1)}, f32[2,16,1280]{2,1,0:T(8,128)S(1)}, u32[]{:S(2)}, u32[]{:S(2)}) collective-permute-start(f32[2,16,1280]{2,1,0:T(8,128)S(1)} %get-tuple-element.61), channel_id=1, source_target_pairs={{0,4},{4,0},{8,12},{12,8},{1,5},{5,1},{9,13},{13,9},{2,6},{6,2},{1... | collective-permute-start | bytes 491528 | tf_op jit(solution)/shard_map/ppermute | solution.py:677
  11.1 29.4 %collective-permute-start.7 = (bf16[2,512,512]{2,1,0:T(8,128)(2,1)S(1)}, bf16[2,512,512]{2,1,0:T(8,128)(2,1)S(1)}, u32[]{:S(2)}, u32[]{:S(2)}) collective-permute-start(bf16[2,512,512]{2,1,0:T(8,128)(2,1)S(1)} %copy-done.4), channel_id=1, source_target_pairs={{0,1},{1,0},{2,3},{3,2},{4,5},{5,4},{6,7},{7,6},{8,9},{9,8},{10,11... | collective-permute-start | bytes 3145736 | tf_op jit(solution)/shard_map/ppermute | solution.py:674
  11.1 29.4 %collective-permute-start.8 = (bf16[2,512,512]{2,1,0:T(8,128)(2,1)S(1)}, bf16[2,512,512]{2,1,0:T(8,128)(2,1)S(1)}, u32[]{:S(2)}, u32[]{:S(2)}) collective-permute-start(bf16[2,512,512]{2,1,0:T(8,128)(2,1)S(1)} %copy-done.5), channel_id=1, source_target_pairs={{0,1},{1,0},{2,3},{3,2},{4,5},{5,4},{6,7},{7,6},{8,9},{9,8},{10,11... | collective-permute-start | bytes 3145736 | tf_op jit(solution)/shard_map/ppermute | solution.py:674
  15.6 5.7 %collective-permute-start.1 = (f32[2,16,1280]{2,1,0:T(8,128)S(1)}, f32[2,16,1280]{2,1,0:T(8,128)S(1)}, u32[]{:S(2)}, u32[]{:S(2)}) collective-permute-start(f32[2,16,1280]{2,1,0:T(8,128)S(1)} %get-tuple-element.62), channel_id=1, source_target_pairs={{0,4},{4,0},{8,12},{12,8},{1,5},{5,1},{9,13},{13,9},{2,6},{6,2},{1... | collective-permute-start | bytes 491528 | tf_op jit(solution)/shard_map/ppermute | solution.py:677
  21.3 9.2 %collective-permute-start.3 = (f32[2,16,1280]{2,1,0:T(8,128)S(1)}, f32[2,16,1280]{2,1,0:T(8,128)S(1)}, u32[]{:S(2)}, u32[]{:S(2)}) collective-permute-start(f32[2,16,1280]{2,1,0:T(8,128)S(1)} %fusion.2), channel_id=1, source_target_pairs={{0,8},{4,12},{8,0},{12,4},{1,9},{5,13},{9,1},{13,5},{2,10},{6,14},... | collective-permute-start | bytes 491528 | tf_op jit(solution)/shard_map/ppermute | solution.py:677
  30.7 9.1 %collective-permute-start.4 = (bf16[2,2,64,128]{3,2,1,0:T(8,128)(2,1)S(1)}, bf16[2,2,64,128]{3,2,1,0:T(8,128)(2,1)S(1)}, u32[]{:S(2)}, u32[]{:S(2)}) collective-permute-start(bf16[2,2,64,128]{3,2,1,0:T(8,128)(2,1)S(1)} %get-tuple-element.39.q_ref.refs_0_), channel_id=1, source_target_pairs={{0,4},{4,0},{8,12},{12,8},{1,5},{5,1},{9,13},{13,9},{2,6},{6,2},{1... | collective-permute-start | bytes 196616 | tf_op jit(solution)/shard_map/ppermute | solution.py:677
  31.0 8.8 %collective-permute-start.5 = (bf16[2,2,64,128]{3,2,1,0:T(8,128)(2,1)S(1)}, bf16[2,2,64,128]{3,2,1,0:T(8,128)(2,1)S(1)}, u32[]{:S(2)}, u32[]{:S(2)}) collective-permute-start(bf16[2,2,64,128]{3,2,1,0:T(8,128)(2,1)S(1)} %get-tuple-element.39.q_ref.refs_0_), channel_id=1, source_target_pairs={{0,8},{4,12},{8,0},{12,4},{1,9},{5,13},{9,1},{13,5},{2,10},{6,14},... | collective-permute-start | bytes 196616 | tf_op jit(solution)/shard_map/ppermute | solution.py:677
  34.4 6.1 %collective-permute-start.6 = (bf16[2,2,64,128]{3,2,1,0:T(8,128)(2,1)S(1)}, bf16[2,2,64,128]{3,2,1,0:T(8,128)(2,1)S(1)}, u32[]{:S(2)}, u32[]{:S(2)}) collective-permute-start(bf16[2,2,64,128]{3,2,1,0:T(8,128)(2,1)S(1)} %get-tuple-element.39.q_ref.refs_0_), channel_id=1, source_target_pairs={{0,12},{4,8},{8,4},{12,0},{1,13},{5,9},{9,5},{13,1},{2,14},{6,10},... | collective-permute-start | bytes 196616 | tf_op jit(solution)/shard_map/ppermute | solution.py:677
  35.2 26.1 %slice-start = ((s8[8388608]{0:T(1024)(128)(4,1)}), s8[4194304]{0:T(1024)(128)(4,1)S(1)}, s32[]{:S(2)}) async-start(s8[8388608]{0:T(1024)(128)(4,1)} %bitcast.10), calls=%async_computation | async-start | bytes 8388608
  37.2 3.3 %copy-start.1 = (s32[8]{0:T(128)S(1)}, s32[8]{0:T(128)}, u32[]{:S(2)}) copy-start(s32[8]{0:T(128)} %prompts.1) | copy-start | bytes 100
  37.2 24.0 %slice-start.1 = ((s8[8388608]{0:T(1024)(128)(4,1)}), s8[4194304]{0:T(1024)(128)(4,1)S(1)}, s32[]{:S(2)}) async-start(s8[8388608]{0:T(1024)(128)(4,1)} %bitcast.10), calls=%async_computation.1 | async-start | bytes 8388608
  43.3 4.7 %collective-permute-start.11 = (bf16[320,128]{1,0:T(8,128)(2,1)S(1)}, bf16[320,128]{1,0:T(8,128)(2,1)S(1)}, u32[]{:S(2)}, u32[]{:S(2)}) collective-permute-start(bf16[320,128]{1,0:T(8,128)(2,1)S(1)} %get-tuple-element.56), channel_id=1, source_target_pairs={{0,4},{4,0},{8,12},{12,8},{1,5},{5,1},{9,13},{13,9},{2,6},{6,2},{1... | collective-permute-start | bytes 245768 | tf_op jit(solution)/shard_map/ppermute | solution.py:677
  43.4 7.2 %collective-permute-start.12 = (bf16[320,128]{1,0:T(8,128)(2,1)S(1)}, bf16[320,128]{1,0:T(8,128)(2,1)S(1)}, u32[]{:S(2)}, u32[]{:S(2)}) collective-permute-start(bf16[320,128]{1,0:T(8,128)(2,1)S(1)} %get-tuple-element.57), channel_id=1, source_target_pairs={{0,8},{4,12},{8,0},{12,4},{1,9},{5,13},{9,1},{13,5},{2,10},{6,14},... | collective-permute-start | bytes 245768 | tf_op jit(solution)/shard_map/ppermute | solution.py:677
  46.5 6.3 %collective-permute-start.13 = (bf16[320,128]{1,0:T(8,128)(2,1)S(1)}, bf16[320,128]{1,0:T(8,128)(2,1)S(1)}, u32[]{:S(2)}, u32[]{:S(2)}) collective-permute-start(bf16[320,128]{1,0:T(8,128)(2,1)S(1)} %get-tuple-element.58), channel_id=1, source_target_pairs={{0,12},{4,8},{8,4},{12,0},{1,13},{5,9},{9,5},{13,1},{2,14},{6,10},... | collective-permute-start | bytes 245768 | tf_op jit(solution)/shard_map/ppermute | solution.py:677
  53.1 4.5 %collective-permute-start.15 = (bf16[16,2048]{1,0:T(8,128)(2,1)S(1)}, bf16[16,2048]{1,0:T(8,128)(2,1)S(1)}, u32[]{:S(2)}, u32[]{:S(2)}) collective-permute-start(bf16[16,2048]{1,0:T(8,128)(2,1)S(1)} %merge.1.refs_0_), channel_id=1, source_target_pairs={{0,4},{4,0},{8,12},{12,8},{1,5},{5,1},{9,13},{13,9},{2,6},{6,2},{1... | collective-permute-start | bytes 196616 | tf_op jit(solution)/shard_map/ppermute | solution.py:677
  53.2 5.2 %collective-permute-start.17 = (bf16[16,2048]{1,0:T(8,128)(2,1)S(1)}, bf16[16,2048]{1,0:T(8,128)(2,1)S(1)}, u32[]{:S(2)}, u32[]{:S(2)}) collective-permute-start(bf16[16,2048]{1,0:T(8,128)(2,1)S(1)} %merge.1.refs_0_), channel_id=1, source_target_pairs={{0,8},{4,12},{8,0},{12,4},{1,9},{5,13},{9,1},{13,5},{2,10},{6,14},... | collective-permute-start | bytes 196616 | tf_op jit(solution)/shard_map/ppermute | solution.py:677
  55.1 6.1 %collective-permute-start.19 = (bf16[16,2048]{1,0:T(8,128)(2,1)S(1)}, bf16[16,2048]{1,0:T(8,128)(2,1)S(1)}, u32[]{:S(2)}, u32[]{:S(2)}) collective-permute-start(bf16[16,2048]{1,0:T(8,128)(2,1)S(1)} %merge.1.refs_0_), channel_id=1, source_target_pairs={{0,12},{4,8},{8,4},{12,0},{1,13},{5,9},{9,5},{13,1},{2,14},{6,10},... | collective-permute-start | bytes 196616 | tf_op jit(solution)/shard_map/ppermute | solution.py:677
  57.6 4.5 %collective-permute-start.14 = (bf16[16,2048]{1,0:T(8,128)(2,1)S(1)}, bf16[16,2048]{1,0:T(8,128)(2,1)S(1)}, u32[]{:S(2)}, u32[]{:S(2)}) collective-permute-start(bf16[16,2048]{1,0:T(8,128)(2,1)S(1)} %merge.1.refs_0_), channel_id=1, source_target_pairs={{0,1},{1,0},{2,3},{3,2},{4,5},{5,4},{6,7},{7,6},{8,9},{9,8},{10,11... | collective-permute-start | bytes 196616 | tf_op jit(solution)/shard_map/ppermute | solution.py:674
  57.6 4.5 %collective-permute-start.16 = (bf16[16,2048]{1,0:T(8,128)(2,1)S(1)}, bf16[16,2048]{1,0:T(8,128)(2,1)S(1)}, u32[]{:S(2)}, u32[]{:S(2)}) collective-permute-start(bf16[16,2048]{1,0:T(8,128)(2,1)S(1)} %collective-permute-done.15.refs_1_), channel_id=1, source_target_pairs={{0,1},{1,0},{2,3},{3,2},{4,5},{5,4},{6,7},{7,6},{8,9},{9,8},{10,11... | collective-permute-start | bytes 196616 | tf_op jit(solution)/shard_map/ppermute | solution.py:674
  58.4 3.7 %collective-permute-start.18 = (bf16[16,2048]{1,0:T(8,128)(2,1)S(1)}, bf16[16,2048]{1,0:T(8,128)(2,1)S(1)}, u32[]{:S(2)}, u32[]{:S(2)}) collective-permute-start(bf16[16,2048]{1,0:T(8,128)(2,1)S(1)} %collective-permute-done.17.refs_2_), channel_id=1, source_target_pairs={{0,1},{1,0},{2,3},{3,2},{4,5},{5,4},{6,7},{7,6},{8,9},{9,8},{10,11... | collective-permute-start | bytes 196616 | tf_op jit(solution)/shard_map/ppermute | solution.py:674
  61.2 1.3 %collective-permute-start.20 = (bf16[16,2048]{1,0:T(8,128)(2,1)S(1)}, bf16[16,2048]{1,0:T(8,128)(2,1)S(1)}, u32[]{:S(2)}, u32[]{:S(2)}) collective-permute-start(bf16[16,2048]{1,0:T(8,128)(2,1)S(1)} %collective-permute-done.19.refs_3_), channel_id=1, source_target_pairs={{0,1},{1,0},{2,3},{3,2},{4,5},{5,4},{6,7},{7,6},{8,9},{9,8},{10,11... | collective-permute-start | bytes 196616 | tf_op jit(solution)/shard_map/ppermute | solution.py:674
  63.3 4.3 %collective-permute-start.21 = (bf16[32,1024]{1,0:T(8,128)(2,1)S(1)}, bf16[32,1024]{1,0:T(8,128)(2,1)S(1)}, u32[]{:S(2)}, u32[]{:S(2)}) collective-permute-start(bf16[32,1024]{1,0:T(8,128)(2,1)S(1)} %get-tuple-element.60), channel_id=1, source_target_pairs={{0,2},{2,0},{1,3},{3,1},{4,6},{6,4},{5,7},{7,5},{8,10},{10,8},{9,1... | collective-permute-start | bytes 196616 | tf_op jit(solution)/shard_map/ppermute | solution.py:727
